TPU v7x, 32 devices: a whole 2x2x4 slice. The times are simulated.
32 devices in a mesh: dp: 4 (over x, core), mem: 8 (over z, y).
Axes of the slice: x: 2, y: 2, z: 4, core: 2. Of those that a mesh axis runs over, the one named last changes fastest.
Arguments:
- text: bfloat16 [256, 64, 768], P(('dp', 'mem')), may hold values from -6 to 6
- lengths: int32 [256], P(('dp', 'mem')), may hold values from 1 to 64, as said below
- memory: bfloat16 [256, 96, 768], P('dp', 'mem'), may hold values from -6 to 6
- out_grad: bfloat16 [256, 64, 768], P(('dp', 'mem')), may hold values from -6 to 6
- self_query: bfloat16 [768, 768], P('dp', 'mem'), may hold values from -0.21875 to 0.21875
- self_key: bfloat16 [768, 768], P('dp', 'mem'), may hold values from -0.21875 to 0.21875
- self_value: bfloat16 [768, 768], P('dp', 'mem'), may hold values from -0.21875 to 0.21875
- self_output: bfloat16 [768, 768], P('dp', 'mem'), may hold values from -0.5 to 0.5
- cross_query: bfloat16 [768, 768], P('dp', 'mem'), may hold values from -0.21875 to 0.21875
- cross_key: bfloat16 [768, 768], P('dp', 'mem'), may hold values from -0.21875 to 0.21875
- cross_value: bfloat16 [768, 768], P('dp', 'mem'), may hold values from -0.21875 to 0.21875
- cross_output: bfloat16 [768, 768], P('dp', 'mem'), may hold values from -0.75 to 0.75
- hidden_in: bfloat16 [768, 3072], P('dp', 'mem'), may hold values from -0.21875 to 0.21875
- hidden_out: bfloat16 [3072, 768], P('dp', 'mem'), may hold values from -0.109375 to 0.109375
- first_gain: float32 [768], replicated, may hold values from 0.5 to 1.5
- first_shift: float32 [768], replicated, may hold values from -3 to 3
- second_gain: float32 [768], replicated, may hold values from 0.5 to 1.5
- second_shift: float32 [768], replicated, may hold values from -3 to 3
- third_gain: float32 [768], replicated, may hold values from 0.5 to 1.5
- third_shift: float32 [768], replicated, may hold values from -3 to 3
Outputs:
- layer_out: bfloat16 [256, 64, 768], P(('dp', 'mem'))
- text_grad: bfloat16 [256, 64, 768], P(('dp', 'mem'))
- memory_grad: bfloat16 [256, 96, 768], P('dp', 'mem')
- self_query_grad: float32 [768, 768], P('dp', 'mem')
- self_key_grad: float32 [768, 768], P('dp', 'mem')
- self_value_grad: float32 [768, 768], P('dp', 'mem')
- self_output_grad: float32 [768, 768], P('dp', 'mem')
- cross_query_grad: float32 [768, 768], P('dp', 'mem')
- cross_key_grad: float32 [768, 768], P('dp', 'mem')
- cross_value_grad: float32 [768, 768], P('dp', 'mem')
- cross_output_grad: float32 [768, 768], P('dp', 'mem')
- hidden_in_grad: float32 [768, 3072], P('dp', 'mem')
- hidden_out_grad: float32 [3072, 768], P('dp', 'mem')
- first_gain_grad: float32 [768], replicated
- first_shift_grad: float32 [768], replicated
- second_gain_grad: float32 [768], replicated
- second_shift_grad: float32 [768], replicated
- third_gain_grad: float32 [768], replicated
- third_shift_grad: float32 [768], replicated
Inputs may be any that keep to these rules, and one draw needn't show every extreme that they name: `lengths`: each image's caption length; slots at and beyond it are padding; some image has 64 and some has 1.
All inputs are finite; a program needn't handle non-finite values.
Results may differ from a plain program's by a relative error of at most 0.023.
Values may be sent and summed in bfloat16 or wider, within the bound.
A program may use at most 192 MiB of HBM per device.

v0:
```python
import functools

import jax
import jax.numpy as jnp
from jax import lax
from jax.experimental import pallas as pl
from jax.experimental.pallas import tpu as pltpu
from jax.sharding import PartitionSpec as P

HEADS = 12
HEAD = 64
MESH = pl.DeviceIdType.MESH
BF = jnp.bfloat16
F32 = jnp.float32
EPS = 1e-06
NEG = -1e30


def layer_norm(values, scaling, offsets):
    center = values - jnp.mean(values, axis=-1, keepdims=True)
    spread = jnp.mean(center * center, axis=-1, keepdims=True)
    return center * lax.rsqrt(spread + EPS) * scaling + offsets


def norm_back(values, scaling, offsets, upstream):
    _, pull_back = jax.vjp(layer_norm, values, scaling, offsets)
    return pull_back(upstream)


def split_heads(values):
    return values.reshape(values.shape[0], values.shape[1], HEADS, HEAD)


def join_heads(values):
    return values.reshape(values.shape[0], values.shape[1], HEADS * HEAD)


def apply_mat(acts, matrix):
    return jnp.einsum("bsd,de->bse", acts, matrix, preferred_element_type=jnp.float32)


def apply_back(grads, matrix):
    return jnp.einsum("bse,de->bsd", grads, matrix, preferred_element_type=jnp.float32)


def mat_grad(acts, grads):
    return jnp.einsum("bsd,bse->de", acts, grads, preferred_element_type=jnp.float32)


def score_rows(queries, keys, allowed):
    score_scale = HEAD ** (-0.5)
    scores = (
        jnp.einsum(
            "bshd,bthd->bhst",
            split_heads(queries),
            split_heads(keys),
            preferred_element_type=jnp.float32,
        )
        * score_scale
    )
    if allowed is not None:
        scores = jnp.where(allowed, scores, NEG)
    return scores


def attend_fwd(queries, keys, values, allowed):
    scores = score_rows(queries, keys, allowed)
    highest = jnp.max(scores, axis=-1, keepdims=True)
    powered = jnp.exp(scores - highest)
    expo_sum = jnp.sum(powered, axis=-1, keepdims=True)
    weights = (powered / expo_sum).astype(jnp.bfloat16)
    mixed_heads = jnp.einsum(
        "bhst,bthd->bshd", weights, split_heads(values), preferred_element_type=jnp.float32
    )
    return (join_heads(mixed_heads).astype(jnp.bfloat16), highest + jnp.log(expo_sum))


def attend_back(queries, keys, values, allowed, log_sum, upstream):
    score_scale = HEAD ** (-0.5)
    probs_full = jnp.exp(score_rows(queries, keys, allowed) - log_sum)
    heads_up = split_heads(upstream)
    prob_grad = jnp.einsum(
        "bshd,bthd->bhst", heads_up, split_heads(values), preferred_element_type=jnp.float32
    )
    score_low = (
        probs_full * (prob_grad - jnp.sum(prob_grad * probs_full, axis=-1, keepdims=True))
    ).astype(jnp.bfloat16)
    value_grad = jnp.einsum(
        "bhst,bshd->bthd",
        probs_full.astype(jnp.bfloat16),
        heads_up,
        preferred_element_type=jnp.float32,
    )
    query_grad = (
        jnp.einsum(
            "bhst,bthd->bshd", score_low, split_heads(keys), preferred_element_type=jnp.float32
        )
        * score_scale
    )
    key_grad = (
        jnp.einsum(
            "bhst,bshd->bthd", score_low, split_heads(queries), preferred_element_type=jnp.float32
        )
        * score_scale
    )
    return (
        join_heads(query_grad).astype(jnp.bfloat16),
        join_heads(key_grad).astype(jnp.bfloat16),
        join_heads(value_grad).astype(jnp.bfloat16),
    )


def fetch_weights(mats):
    columns = (
        lax.all_gather(mats[0], "mem", axis=1, tiled=True),
        lax.all_gather(mats[1], "mem", axis=1, tiled=True),
        lax.all_gather(mats[2], "mem", axis=1, tiled=True),
        lax.all_gather(mats[3], "mem", axis=1, tiled=True),
        lax.all_gather(mats[4], "mem", axis=1, tiled=True),
        lax.all_gather(mats[5], "mem", axis=1, tiled=True),
        lax.all_gather(mats[6], "mem", axis=1, tiled=True),
        lax.all_gather(mats[7], "mem", axis=1, tiled=True),
        lax.all_gather(mats[8], "mem", axis=1, tiled=True),
        lax.all_gather(mats[9], "mem", axis=1, tiled=True),
    )
    return (
        lax.all_gather(columns[0], "dp", axis=0, tiled=True),
        lax.all_gather(columns[1], "dp", axis=0, tiled=True),
        lax.all_gather(columns[2], "dp", axis=0, tiled=True),
        lax.all_gather(columns[3], "dp", axis=0, tiled=True),
        lax.all_gather(columns[4], "dp", axis=0, tiled=True),
        lax.all_gather(columns[5], "dp", axis=0, tiled=True),
        lax.all_gather(columns[6], "dp", axis=0, tiled=True),
        lax.all_gather(columns[7], "dp", axis=0, tiled=True),
        lax.all_gather(columns[8], "dp", axis=0, tiled=True),
        lax.all_gather(columns[9], "dp", axis=0, tiled=True),
    )


def reduce_all(grads):
    row_sums = (
        lax.psum_scatter(
            grads[0].astype(jnp.bfloat16), "dp", scatter_dimension=0, tiled=True
        ).astype(jnp.float32),
        lax.psum_scatter(
            grads[1].astype(jnp.bfloat16), "dp", scatter_dimension=0, tiled=True
        ).astype(jnp.float32),
        lax.psum_scatter(
            grads[2].astype(jnp.bfloat16), "dp", scatter_dimension=0, tiled=True
        ).astype(jnp.float32),
        lax.psum_scatter(
            grads[3].astype(jnp.bfloat16), "dp", scatter_dimension=0, tiled=True
        ).astype(jnp.float32),
        lax.psum_scatter(
            grads[4].astype(jnp.bfloat16), "dp", scatter_dimension=0, tiled=True
        ).astype(jnp.float32),
        lax.psum_scatter(
            grads[5].astype(jnp.bfloat16), "dp", scatter_dimension=0, tiled=True
        ).astype(jnp.float32),
        lax.psum_scatter(
            grads[6].astype(jnp.bfloat16), "dp", scatter_dimension=0, tiled=True
        ).astype(jnp.float32),
        lax.psum_scatter(
            grads[7].astype(jnp.bfloat16), "dp", scatter_dimension=0, tiled=True
        ).astype(jnp.float32),
        lax.psum_scatter(
            grads[8].astype(jnp.bfloat16), "dp", scatter_dimension=0, tiled=True
        ).astype(jnp.float32),
        lax.psum_scatter(
            grads[9].astype(jnp.bfloat16), "dp", scatter_dimension=0, tiled=True
        ).astype(jnp.float32),
    )
    return (
        lax.psum_scatter(
            row_sums[0].astype(jnp.bfloat16), "mem", scatter_dimension=1, tiled=True
        ).astype(jnp.float32),
        lax.psum_scatter(
            row_sums[1].astype(jnp.bfloat16), "mem", scatter_dimension=1, tiled=True
        ).astype(jnp.float32),
        lax.psum_scatter(
            row_sums[2].astype(jnp.bfloat16), "mem", scatter_dimension=1, tiled=True
        ).astype(jnp.float32),
        lax.psum_scatter(
            row_sums[3].astype(jnp.bfloat16), "mem", scatter_dimension=1, tiled=True
        ).astype(jnp.float32),
        lax.psum_scatter(
            row_sums[4].astype(jnp.bfloat16), "mem", scatter_dimension=1, tiled=True
        ).astype(jnp.float32),
        lax.psum_scatter(
            row_sums[5].astype(jnp.bfloat16), "mem", scatter_dimension=1, tiled=True
        ).astype(jnp.float32),
        lax.psum_scatter(
            row_sums[6].astype(jnp.bfloat16), "mem", scatter_dimension=1, tiled=True
        ).astype(jnp.float32),
        lax.psum_scatter(
            row_sums[7].astype(jnp.bfloat16), "mem", scatter_dimension=1, tiled=True
        ).astype(jnp.float32),
        lax.psum_scatter(
            row_sums[8].astype(jnp.bfloat16), "mem", scatter_dimension=1, tiled=True
        ).astype(jnp.float32),
        lax.psum_scatter(
            row_sums[9].astype(jnp.bfloat16), "mem", scatter_dimension=1, tiled=True
        ).astype(jnp.float32),
    )


def shards(
    text,
    lengths,
    memory,
    out_grad,
    self_query,
    self_key,
    self_value,
    self_output,
    cross_query,
    cross_key,
    cross_value,
    cross_output,
    hidden_in,
    hidden_out,
    first_gain,
    first_shift,
    second_gain,
    second_shift,
    third_gain,
    third_shift,
):
    mats = (
        self_query,
        self_key,
        self_value,
        self_output,
        cross_query,
        cross_key,
        cross_value,
        cross_output,
        hidden_in,
        hidden_out,
    )
    full_mats = fetch_weights(mats)
    w_query, w_key, w_value, w_output, m_query, m_key, m_value, m_output, w_in, w_out = full_mats
    places = jnp.arange(text.shape[1])
    valid_row = places[None, :] < lengths[:, None]
    allowed = (places[None, :] <= places[:, None])[None, None] & valid_row[:, None, None, :]
    residual = text.astype(jnp.float32)
    first = layer_norm(residual, first_gain, first_shift).astype(jnp.bfloat16)
    queries = apply_mat(first, w_query).astype(jnp.bfloat16)
    keys = apply_mat(first, w_key).astype(jnp.bfloat16)
    values = apply_mat(first, w_value).astype(jnp.bfloat16)
    self_mixed, self_lse = attend_fwd(queries, keys, values, allowed)
    after_self = residual + apply_mat(self_mixed, w_output)
    memory_rows = lax.all_to_all(memory, "mem", split_axis=0, concat_axis=1, tiled=True)
    second = layer_norm(after_self, second_gain, second_shift).astype(jnp.bfloat16)
    cross_queries = apply_mat(second, m_query).astype(jnp.bfloat16)
    mem_keys = apply_mat(memory_rows, m_key).astype(jnp.bfloat16)
    mem_values = apply_mat(memory_rows, m_value).astype(jnp.bfloat16)
    cross_mixed, cross_lse = attend_fwd(cross_queries, mem_keys, mem_values, None)
    after_cross = after_self + apply_mat(cross_mixed, m_output)
    third = layer_norm(after_cross, third_gain, third_shift).astype(jnp.bfloat16)
    before_act = apply_mat(third, w_in)
    activated = jax.nn.gelu(before_act).astype(jnp.bfloat16)
    final = after_cross + apply_mat(activated, w_out)
    layer_out = jnp.where(valid_row[:, :, None], final, 0.0).astype(jnp.bfloat16)
    b_query, b_key, b_value, b_output, n_query, n_key, n_value, n_output, b_in, b_out = full_mats
    grad_top = jnp.where(valid_row[:, :, None], out_grad.astype(jnp.float32), 0.0)
    top_low = grad_top.astype(jnp.bfloat16)
    hidden_out_grad = mat_grad(activated, top_low)
    _, gelu_pull = jax.vjp(jax.nn.gelu, before_act)
    act_low = gelu_pull(apply_back(top_low, b_out))[0].astype(jnp.bfloat16)
    hidden_in_grad = mat_grad(third, act_low)
    cross_input, third_gain_grad, third_shift_grad = norm_back(
        after_cross, third_gain, third_shift, apply_back(act_low, b_in)
    )
    grad_cross = grad_top + cross_input
    cross_low = grad_cross.astype(jnp.bfloat16)
    cross_output_grad = mat_grad(cross_mixed, cross_low)
    mixed_up = apply_back(cross_low, n_output).astype(jnp.bfloat16)
    cross_query_low, mem_key_low, mem_value_low = attend_back(
        cross_queries, mem_keys, mem_values, None, cross_lse, mixed_up
    )
    cross_query_grad = mat_grad(second, cross_query_low)
    cross_key_grad = mat_grad(memory_rows, mem_key_low)
    cross_value_grad = mat_grad(memory_rows, mem_value_low)
    mem_back = (apply_back(mem_key_low, n_key) + apply_back(mem_value_low, n_value)).astype(
        jnp.bfloat16
    )
    memory_grad = lax.all_to_all(mem_back, "mem", split_axis=1, concat_axis=0, tiled=True)
    self_input, second_gain_grad, second_shift_grad = norm_back(
        after_self, second_gain, second_shift, apply_back(cross_query_low, n_query)
    )
    grad_self = grad_cross + self_input
    self_low = grad_self.astype(jnp.bfloat16)
    self_output_grad = mat_grad(self_mixed, self_low)
    self_up = apply_back(self_low, b_output).astype(jnp.bfloat16)
    query_low, key_low, value_low = attend_back(queries, keys, values, allowed, self_lse, self_up)
    self_query_grad = mat_grad(first, query_low)
    self_key_grad = mat_grad(first, key_low)
    self_value_grad = mat_grad(first, value_low)
    first_up = (
        apply_back(query_low, b_query) + apply_back(key_low, b_key) + apply_back(value_low, b_value)
    )
    text_input, first_gain_grad, first_shift_grad = norm_back(
        residual, first_gain, first_shift, first_up
    )
    text_grad = (grad_self + text_input).astype(jnp.bfloat16)
    weight_sums = reduce_all(
        (
            self_query_grad,
            self_key_grad,
            self_value_grad,
            self_output_grad,
            cross_query_grad,
            cross_key_grad,
            cross_value_grad,
            cross_output_grad,
            hidden_in_grad,
            hidden_out_grad,
        )
    )
    norm_sums = lax.psum(
        (
            first_gain_grad,
            first_shift_grad,
            second_gain_grad,
            second_shift_grad,
            third_gain_grad,
            third_shift_grad,
        ),
        ("dp", "mem"),
    )
    return (
        layer_out,
        text_grad,
        memory_grad,
        weight_sums[0],
        weight_sums[1],
        weight_sums[2],
        weight_sums[3],
        weight_sums[4],
        weight_sums[5],
        weight_sums[6],
        weight_sums[7],
        weight_sums[8],
        weight_sums[9],
        norm_sums[0],
        norm_sums[1],
        norm_sums[2],
        norm_sums[3],
        norm_sums[4],
        norm_sums[5],
    )


class Place:
    def __init__(self):
        self.d = lax.axis_index("dp")
        self.m = lax.axis_index("mem")
        self.c = lax.rem(self.d, 2)
        self.x = lax.div(self.d, 2)
        self.y = lax.rem(self.m, 2)
        self.z = lax.div(self.m, 2)
        self.oc, self.ox, self.oy = 1 - self.c, 1 - self.x, 1 - self.y
        self.sib = (self.x * 2 + self.oc, self.m)
        self.xn = (self.ox * 2 + self.c, self.m)
        self.yn = (self.d, self.z * 2 + self.oy)
        self.xyn = (self.ox * 2 + self.c, self.z * 2 + self.oy)

    def zup(self, k):
        return lax.rem(self.z + k, 4)

    def zpeer(self, k):
        return (self.d, self.zup(k) * 2 + self.y)

    def mpeer(self, k):
        return (self.d, lax.rem(self.m + k, 8))


def greet(at):
    barrier = pltpu.get_barrier_semaphore()
    peers = [at.sib, at.xn, at.xyn] + [at.mpeer(k) for k in range(1, 8)]
    for peer in peers:
        pl.semaphore_signal(barrier, inc=1, device_id=peer, device_id_type=MESH)
    pl.semaphore_wait(barrier, len(peers))


def remote(src, dst, send, recv, peer):
    return pltpu.make_async_remote_copy(
        src_ref=src,
        dst_ref=dst,
        send_sem=send,
        recv_sem=recv,
        device_id=peer,
        device_id_type=MESH,
    )


class Gather:
    SENDS, RECVS = 3, 8

    def __init__(self, at, full, span, via_y, sends, recvs, index):
        self.at, self.full, self.span = at, full, span
        self.sends = [sends.at[self.SENDS * index + i] for i in range(self.SENDS)]
        self.recvs = [recvs.at[self.RECVS * index + i] for i in range(self.RECVS)]
        self.lanes = full.shape[-1] // 2
        self.cuts = ((0, via_y), (via_y, self.lanes - via_y))

    def piece(self, z, y, h, x, cut=None):
        start, size = cut or (0, self.lanes)
        lo = pl.multiple_of(x * self.lanes + start, 128)
        return self.full.at[self.span, z, y, h, :, pl.ds(lo, size)]

    def send(self, kind, slot, ref, peer):
        remote(ref, ref, self.sends[kind], self.recvs[slot], peer).start()

    def got(self, slot, ref):
        remote(ref, ref, self.sends[0], self.recvs[slot], self.at.sib).wait_recv()

    def begin(self):
        at = self.at
        own = self.piece(at.z, at.y, at.c, at.x)
        for k in (1, 2, 3):
            self.send(2, k - 1, own, at.zpeer(k))
        self.send(1, 3, own, at.xn)
        self.send(1, 4, own, at.yn)
        self.send(0, 7, own, at.sib)

    def second(self, k):
        at = self.at
        ref = self.piece(at.zup(4 - k), at.y, at.c, at.x)
        self.got(k - 1, ref)
        self.send(1, 3, ref, at.xn)
        self.send(1, 4, ref, at.yn)
        self.send(0, 7, ref, at.sib)

    def third(self, part):
        at, every = self.at, slice(None)
        x, y, peer = ((at.ox, at.y, at.yn), (at.x, at.oy, at.xn))[part]
        ref = self.piece(every, y, at.c, x)
        self.got(3 + part, ref)
        self.send(1, 5 + part, self.piece(every, y, at.c, x, self.cuts[part]), peer)
        self.send(0, 7, ref, at.sib)

    def fourth(self):
        at = self.at
        for part, cut in enumerate(self.cuts):
            ref = self.piece(slice(None), at.oy, at.c, at.ox, cut)
            self.got(5 + part, ref)
            self.send(0, 7, ref, at.sib)

    def last(self):
        self.got(7, self.full.at[self.span, :, :, self.at.oc])

    def drain(self):
        at = self.at
        for kind, ref in enumerate(
            (
                self.full.at[self.span, :, :, at.c],
                self.full.at[self.span, pl.ds(0, 3), :, at.c],
                self.piece(pl.ds(0, 3), at.y, at.c, at.x),
            )
        ):
            remote(ref, ref, self.sends[kind], self.recvs[0], at.sib).wait_send()


class Reduce:
    RECVS = 7

    def __init__(self, at, full, span, bufs, sends, recvs, index):
        self.at, self.full, self.span = at, full, span
        self.chip, self.via_y, self.via_x, self.rx, self.ry, self.rz, self.fin = bufs
        self.sent = sends.at[index]
        self.recvs = [recvs.at[self.RECVS * index + i] for i in range(self.RECVS)]
        self.count, self.lanes = self.chip.shape[0], full.shape[-1] // 2
        cut = self.via_y.shape[-1]
        self.cuts = (slice(0, cut), slice(cut, self.lanes))

    def send(self, slot, src, dst, peer):
        remote(src, dst, self.sent, self.recvs[slot], peer).start()

    def got(self, slot, ref):
        remote(ref, ref, self.sent, self.recvs[slot], self.at.sib).wait_recv()

    def begin(self):
        at = self.at
        for x in range(2):
            lanes = slice(x * self.lanes, (x + 1) * self.lanes)
            src = self.full.at[self.span, :, :, at.oc, :, lanes]
            self.send(0, src, self.chip.at[:, x], at.sib)

    def second(self):
        at = self.at
        chip, full, lanes, w0 = self.chip, self.full, self.lanes, self.span.start
        self.got(0, chip)

        def add(i, carry):
            w, r = lax.div(i, 8), lax.rem(i, 8)
            z, y = lax.div(r, 2), lax.rem(r, 2)
            for x in range(2):
                mine = full[w0 + w, z, y, at.c, :, x * lanes : (x + 1) * lanes]
                chip[w, x, z, y] = (
                    chip[w, x, z, y].astype(F32) + mine.astype(F32)
                ).astype(BF)
            return carry

        lax.fori_loop(0, 8 * self.count, add, 0)
        self.send(1, chip.at[:, at.ox, :, at.oy, :, self.cuts[0]], self.via_y, at.yn)
        self.send(2, chip.at[:, at.ox, :, at.oy, :, self.cuts[1]], self.via_x, at.xn)

    def third(self, part):
        at, chip = self.at, self.chip
        ref = (self.via_y, self.via_x)[part]
        x, y = ((at.ox, at.y), (at.x, at.oy))[part]
        cut = self.cuts[part]
        self.got(1 + part, ref)

        def add(i, carry):
            w, z = lax.div(i, 4), lax.rem(i, 4)
            chip[w, x, z, y, :, cut] = (
                chip[w, x, z, y, :, cut].astype(F32) + ref[w, z].astype(F32)
            ).astype(BF)
            return carry

        lax.fori_loop(0, 4 * self.count, add, 0)
        box, peer = ((self.rx, at.xn), (self.ry, at.yn))[part]
        self.send(3 + part, chip.at[:, x, :, y], box, peer)

    def fourth(self):
        at, chip = self.at, self.chip
        self.got(3, self.rx)
        self.got(4, self.ry)

        def add(i, carry):
            w, z = lax.div(i, 4), lax.rem(i, 4)
            chip[w, at.x, z, at.y] = (
                chip[w, at.x, z, at.y].astype(F32)
                + self.rx[w, z].astype(F32)
                + self.ry[w, z].astype(F32)
            ).astype(BF)
            return carry

        lax.fori_loop(0, 4 * self.count, add, 0)
        for k in (1, 2, 3):
            src = chip.at[:, at.x, at.zup(k), at.y]
            self.send(5, src, self.rz.at[k - 1], at.zpeer(k))

    def fifth(self):
        at = self.at
        self.got(5, self.rz)

        def add(w, carry):
            total = self.chip[w, at.x, at.z, at.y].astype(F32)
            for k in range(3):
                total = total + self.rz[k, w].astype(F32)
            self.fin[w, at.c] = total.astype(BF)
            return carry

        lax.fori_loop(0, self.count, add, 0)
        mine = self.fin.at[:, at.c]
        self.send(6, mine, mine, at.sib)

    def last(self):
        self.got(6, self.fin.at[:, self.at.oc])

    def drain(self):
        ref = self.full.at[self.span]
        remote(ref, ref, self.sent, self.recvs[0], self.at.sib).wait_send()


def reduce_bufs(count, rows, lanes, cut):
    return [
        pltpu.VMEM((count, 2, 4, 2, rows, lanes), BF),
        pltpu.VMEM((count, 4, rows, cut), BF),
        pltpu.VMEM((count, 4, rows, lanes - cut), BF),
        pltpu.VMEM((count, 4, rows, lanes), BF),
        pltpu.VMEM((count, 4, rows, lanes), BF),
        pltpu.VMEM((3, count, rows, lanes), BF),
        pltpu.VMEM((count, 2, rows, lanes), BF),
    ]


def pick(rows, cols, start):
    col = lax.broadcasted_iota(jnp.int32, (rows, cols), 1)
    row = lax.broadcasted_iota(jnp.int32, (rows, cols), 0)
    return jnp.where(col == row + start, 1.0, 0.0).astype(BF)


def dot_nt(a, b):
    return lax.dot_general(a, b, (((1,), (1,)), ((), ())), preferred_element_type=F32)


def dot_nn(a, b):
    return lax.dot_general(a, b, (((1,), (0,)), ((), ())), preferred_element_type=F32)


def dot_tn(a, b):
    return lax.dot_general(a, b, (((0,), (0,)), ((), ())), preferred_element_type=F32)


def norm_stats(values):
    center = values - jnp.mean(values, axis=-1, keepdims=True)
    scale = lax.rsqrt(jnp.mean(center * center, axis=-1, keepdims=True) + EPS)
    return center * scale, scale


def gelu_both(value):
    c0, c1 = 0.7978845608028654, 0.044715
    square = value * value
    tanh = jnp.tanh(c0 * value * (1.0 + c1 * square))
    half = 0.5 + 0.5 * tanh
    slope = half + 0.5 * value * (1.0 - tanh * tanh) * (c0 + 3.0 * c0 * c1 * square)
    return value * half, slope


def softmax(scores):
    powered = jnp.exp(scores - jnp.max(scores, axis=-1, keepdims=True))
    return powered / jnp.sum(powered, axis=-1, keepdims=True)


class Layer:
    def __init__(self, **refs):
        self.__dict__.update(refs)
        self.tokens, self.dmodel = self.nrm.shape
        self.images = self.own_images
        self.txt = self.tokens // self.images
        self.mem_len = self.mkv.shape[1] // self.images
        lane = lax.broadcasted_iota(jnp.int32, (1, 4 * HEAD), 1)
        self.head_lanes = [
            jnp.where((lane >= HEAD * h) & (lane < HEAD * (h + 1)), 1.0, 0.0)
            for h in range(4)
        ]

    def weight(self, i):
        return self.full_s[i].reshape(self.dmodel, self.dmodel)

    def put_weight(self, i, value):
        self.full_s[i] = value.astype(BF).reshape(self.full_s.shape[1:])

    def blocks(self, size, fn, total=None):
        def step(i, carry):
            fn(pl.ds(pl.multiple_of(i * size, size), size))
            return carry

        lax.fori_loop(0, (total or self.tokens) // size, step, 0)

    def spread(self, value):
        return jnp.concatenate(
            [value * mask.astype(BF) for mask in self.head_lanes], axis=0
        )

    def gather_heads(self, value):
        n = value.shape[0] // 4
        out = value[:n] * self.head_lanes[0]
        for h in range(1, 4):
            out = out + value[h * n : (h + 1) * n] * self.head_lanes[h]
        return out

    def norm_into(self, source, index):
        gain, shift = self.norms[2 * index : 2 * index + 1], self.norms[2 * index + 1 : 2 * index + 2]

        def block(rows):
            hat, _ = norm_stats(source[rows, :].astype(F32))
            self.nrm[rows, :] = (hat * gain + shift).astype(BF)

        self.blocks(128, block)

    def norm_back(self, source, upstream, index, finish):
        gain = self.norms[2 * index : 2 * index + 1]

        def step(i, carry):
            rows = pl.ds(pl.multiple_of(i * 64, 64), 64)
            hat, scale = norm_stats(source[rows, :].astype(F32))
            up = upstream[rows, :]
            scaled = up * gain
            first = jnp.mean(scaled, axis=-1, keepdims=True)
            second = jnp.mean(scaled * hat, axis=-1, keepdims=True)
            finish(rows, scale * (scaled - first - hat * second))
            gains, shifts = carry
            return (
                gains + jnp.sum(up * hat, axis=0, keepdims=True),
                shifts + jnp.sum(up, axis=0, keepdims=True),
            )

        zero = jnp.zeros((1, self.dmodel), F32)
        gains, shifts = lax.fori_loop(0, self.tokens // 64, step, (zero, zero))
        self.norm_grads[2 * index : 2 * index + 1, :] = gains
        self.norm_grads[2 * index + 1 : 2 * index + 2, :] = shifts


    def project(self, outs, value, first):
        def step(i, carry):
            outs[i] = dot_nt(value(), self.weight(first + i)).astype(BF)
            return carry

        lax.fori_loop(0, outs.shape[0], step, 0)

    def allowed(self, p):
        n = 2 * self.txt
        row = lax.broadcasted_iota(jnp.int32, (n, n), 0)
        col = lax.broadcasted_iota(jnp.int32, (n, n), 1)
        late = col >= self.txt
        length = jnp.where(
            late, self.txt + self.lengths[2 * p + 1], self.lengths[2 * p]
        )
        return (col <= row) & (col < length) & (late == (row >= self.txt))

    def self_forward(self, start, stop):
        def pair(p, carry):
            rows = pl.ds(pl.multiple_of(p * 128, 128), 128)
            allow = self.allowed(p)
            for g in range(self.dmodel // 256):
                cols = slice(256 * g, 256 * g + 256)
                scores = dot_nt(self.spread(self.qkv[0, rows, cols]), self.qkv[1, rows, cols])
                scores = scores.reshape(4, 128, 128) * HEAD**-0.5
                scores = jnp.where(allow[None], scores, NEG)
                probs = softmax(scores).reshape(512, 128).astype(BF)
                self.ps[p, g] = probs
                mixed = dot_nn(probs, self.qkv[2, rows, cols])
                self.sm[rows, cols] = self.gather_heads(mixed).astype(BF)
            return carry

        lax.fori_loop(start, stop, pair, 0)

    def add_after_self(self):
        def block(rows):
            self.after_self[rows, :] = self.io[rows, :].astype(F32) + dot_nt(
                self.sm[rows, :], self.weight(3)
            )

        self.blocks(256, block)

    def memory_in(self):
        n, size = self.images, self.mem_len
        total = n * size

        def block(i, carry):
            row = lax.broadcasted_iota(jnp.int32, (size, total), 0)
            col = lax.broadcasted_iota(jnp.int32, (size, total), 1)
            hot = jnp.where(col == n * row + i, 1.0, 0.0).astype(BF)
            rows = pl.ds(pl.multiple_of(i * size, 32), size)
            self.mkv[0, rows, :] = dot_nn(hot, self.memory()).astype(BF)
            return carry

        lax.fori_loop(0, n, block, 0)
        self.rows[...] = self.mkv[0].reshape(self.rows.shape)

    def memory(self):
        return self.rows[...].reshape(self.mkv.shape[1:])

    def memory_out(self):
        n, size = self.images, self.mem_len
        short, total = size // n, n * size

        def block(b, carry):
            row = lax.broadcasted_iota(jnp.int32, (size, total), 0)
            col = lax.broadcasted_iota(jnp.int32, (size, total), 1)
            image = row & (n - 1)
            slot = lax.shift_right_logical(row, n.bit_length() - 1) + b * short
            hot = jnp.where(col == image * size + slot, 1.0, 0.0).astype(BF)
            low, high = self.cm[...], self.t2[: total - self.tokens, : self.dmodel]
            back = dot_nn(hot[:, : self.tokens], low) + dot_nn(hot[:, self.tokens :], high)
            self.rows[b] = back.astype(BF).reshape(self.rows.shape[1:])
            return carry

        lax.fori_loop(0, n, block, 0)

    def probs_at(self, i, g):
        size = 4 * self.txt
        start = pl.multiple_of(lax.rem(i, 2) * size, size)
        return lax.div(i, 2), g, pl.ds(start, size), slice(0, self.mem_len)

    def cross_forward(self, start, stop):
        def image(i, carry):
            rows = pl.ds(pl.multiple_of(i * self.txt, 64), self.txt)
            mems = pl.ds(pl.multiple_of(i * self.mem_len, 32), self.mem_len)
            for g in range(self.dmodel // 256):
                cols = slice(256 * g, 256 * g + 256)
                scores = dot_nt(self.spread(self.cq[0, rows, cols]), self.mkv[0, mems, cols])
                probs = softmax(scores * HEAD**-0.5).astype(BF)
                self.ps[self.probs_at(i, g)] = probs
                mixed = dot_nn(probs, self.mkv[1, mems, cols])
                self.cm[rows, cols] = self.gather_heads(mixed).astype(BF)
            return carry

        lax.fori_loop(start, stop, image, 0)

    def add_after_cross(self):
        def block(rows):
            self.after_cross[rows, :] = self.after_self[rows, :] + dot_nt(
                self.cm[rows, :], self.weight(7)
            )

        self.blocks(256, block)


    def mask_top(self):
        def block(rows):
            self.io[rows, :] = self.io[rows, :] * self.valid[rows, :1]

        self.blocks(128, block)

    def feed_start(self):
        def block(rows):
            self.acc_out[rows, :] = self.after_cross[rows, :]
            self.acc_up[rows, :] = jnp.zeros((128, self.dmodel), F32)

        self.blocks(128, block)

    def feed_chunk(self, s):
        dmodel = self.dmodel
        units = self.t2.shape[1]

        def w_in(lo=0, n=units):
            return self.full_in[s].reshape(units, dmodel)[lo : lo + n]

        def w_out(lo=0, n=units):
            return self.full_out[s, :, :, :, :, lo : lo + n].reshape(dmodel, n)

        def block(rows):
            for lo in range(0, units, 512):
                before = dot_nt(self.nrm[rows, :], w_in(lo, 512))
                act, slope = gelu_both(before)
                self.t2[rows, lo : lo + 512] = act.astype(BF)
                up = dot_nn(self.io[rows, :], w_out(lo, 512))
                self.t3[rows, lo : lo + 512] = (slope * up).astype(BF)

        self.blocks(256, block)

        def block(rows):
            self.acc_out[rows, :] += dot_nt(self.t2[rows, :], w_out())
            self.acc_up[rows, :] += dot_nn(self.t3[rows, :], w_in())

        self.blocks(256, block)
        shape = self.full_out.shape[1:5]
        for lo in range(0, units, 512):
            grad = dot_tn(self.io[...], self.t2[:, lo : lo + 512]).astype(BF)
            self.full_out[s, :, :, :, :, lo : lo + 512] = grad.reshape(shape + (512,))
        grad = dot_tn(self.t3[...], self.nrm[...]).astype(BF)
        self.full_in[s] = grad.reshape(self.full_in.shape[1:])

    def layer_out(self, out):
        def block(rows):
            out[rows, : self.dmodel] = (self.acc_out[rows, :] * self.valid[rows, :1].astype(F32)).astype(BF)

        self.blocks(128, block)


    def third_back(self):
        def finish(rows, grad):
            total = self.io[rows, :].astype(F32) + grad
            self.acc_up[rows, :] = total
            self.io[rows, :] = total.astype(BF)

        self.norm_back(self.after_cross, self.acc_up, 2, finish)

    def output_back(self, i, mixed, out):
        out[:, : self.dmodel] = dot_nn(self.io[...], self.weight(i)).astype(BF)
        self.put_weight(i, dot_tn(self.io[...], mixed[...]))

    def attend_back(self, probs, up, q, k, v, rows, mems, cols):
        low_q = self.spread(q[rows, cols])
        low_up = self.spread(up[rows, cols])
        keys, values = k[mems, cols], v[mems, cols]
        full = probs.astype(F32)
        prob_grad = dot_nt(low_up, values)
        score = full * (prob_grad - jnp.sum(prob_grad * full, axis=-1, keepdims=True))
        score = (score * HEAD**-0.5).astype(BF)
        v[mems, cols] = dot_tn(probs, low_up).astype(BF)
        k[mems, cols] = dot_tn(score, low_q).astype(BF)
        q[rows, cols] = self.gather_heads(dot_nn(score, keys)).astype(BF)

    def cross_back(self, start, stop):
        def image(i, carry):
            rows = pl.ds(pl.multiple_of(i * self.txt, 64), self.txt)
            mems = pl.ds(pl.multiple_of(i * self.mem_len, 32), self.mem_len)
            for g in range(self.dmodel // 256):
                cols = slice(256 * g, 256 * g + 256)
                probs = self.ps[self.probs_at(i, g)]
                self.attend_back(
                    probs,
                    self.t2,
                    self.cq.at[0],
                    self.mkv.at[0],
                    self.mkv.at[1],
                    rows,
                    mems,
                    cols,
                )
            return carry

        lax.fori_loop(start, stop, image, 0)

    def self_back(self, start, stop):
        def pair(p, carry):
            rows = pl.ds(pl.multiple_of(p * 128, 128), 128)
            for g in range(self.dmodel // 256):
                cols = slice(256 * g, 256 * g + 256)
                self.attend_back(
                    self.ps[p, g],
                    self.t2,
                    self.qkv.at[0],
                    self.qkv.at[1],
                    self.qkv.at[2],
                    rows,
                    rows,
                    cols,
                )
            return carry

        lax.fori_loop(start, stop, pair, 0)

    def memory_back(self):
        size = 256
        keys, values = self.mkv.at[0], self.mkv.at[1]

        def back(rows):
            total = dot_nn(keys[rows, :], self.weight(5)) + dot_nn(
                values[rows, :], self.weight(6)
            )
            return total.astype(BF)

        def block(rows):
            self.cm[rows, :] = back(rows)

        self.blocks(size, block)
        for start in range(self.tokens, self.mkv.shape[1], size):
            there = slice(start - self.tokens, start - self.tokens + size)
            self.t2[there, : self.dmodel] = back(slice(start, start + size))

    def weight_grads(self, lows, value, first):
        def step(i, carry):
            self.put_weight(first + i, dot_tn(lows[i], value()))
            return carry

        lax.fori_loop(0, lows.shape[0], step, 0)

    def second_up(self):
        def block(rows):
            self.acc_out[rows, :] = dot_nn(self.cq[0, rows, :], self.weight(4))

        self.blocks(256, block)

    def second_back(self):
        def finish(rows, grad):
            total = self.acc_up[rows, :] + grad
            self.acc_up[rows, :] = total
            self.io[rows, :] = total.astype(BF)

        self.norm_back(self.after_self, self.acc_out, 1, finish)

    def first_up(self):
        def block(rows):
            self.acc_out[rows, :] = (
                dot_nn(self.qkv[0, rows, :], self.weight(0))
                + dot_nn(self.qkv[1, rows, :], self.weight(1))
                + dot_nn(self.qkv[2, rows, :], self.weight(2))
            )

        self.blocks(256, block)

    def first_back(self, text, out):
        def finish(rows, grad):
            out[rows, : self.dmodel] = (self.acc_up[rows, :] + grad).astype(BF)

        self.norm_back(text, self.acc_out, 0, finish)


class NormSum:
    def __init__(self, at, sums, pair, plane, line, out, sends, recvs):
        self.at, self.sums, self.pair = at, sums, pair
        self.boxes = (plane, line)
        self.sends, self.recvs = sends, recvs
        self.me = (at.x * 2 + at.y, at.z)
        self.target = (line.at[at.z], out)
        self.peers = ((at.xn, at.yn, at.xyn), tuple(at.zpeer(k) for k in (1, 2, 3)))
        self.out = []

    def start(self, stage):
        if stage == 0:
            copy = remote(
                self.sums, self.pair, self.sends.at[0], self.recvs.at[0], self.at.sib
            )
            copy.start()
            self.out.append(copy)
            return
        box = self.boxes[stage - 1].at[self.me[stage - 1]]
        for k, peer in enumerate(self.peers[stage - 1]):
            i = 3 * stage - 2 + k
            copy = remote(box, box, self.sends.at[i], self.recvs.at[i], peer)
            copy.start()
            self.out.append(copy)

    def finish(self, stage):
        if stage == 0:
            self.out[0].wait_recv()
            self.boxes[0][self.me[0]] = self.sums[...] + self.pair[...]
            return
        for copy in self.out[3 * stage - 2 : 3 * stage + 1]:
            copy.wait_recv()
        box = self.boxes[stage - 1]
        total = box[0] + box[1] + box[2] + box[3]
        self.target[stage - 1][...] = total


SMALL = ((0, 2), (2, 3), (3, 5), (5, 7), (7, 8))
SMALL_BACK = ((7, 8), (4, 5), (3, 4), (0, 3), (5, 7))
THIRDS = 3
NAMES = ("nrm", "io", "sm", "cm")
WIDE = ("after_self", "after_cross", "acc_out", "acc_up")


def whole_kernel(own_images, *refs):
    refs = list(refs)

    def take(n):
        out = refs[:n]
        del refs[:n]
        return out

    shards, (rows_in, text_in, top_in, lengths), vectors = take(10), take(4), take(6)
    fins, (layer_out, text_out, rows_out, norm_out, spill) = take(3), take(5)
    full_s, full_in, full_out, pair_s, pair_in, pair_out = take(6)
    bufs = [take(7) for _ in range(2 * THIRDS + len(SMALL_BACK))]
    narrow, wide = take(len(NAMES)), take(len(WIDE))
    qkv, cq, mkv, t2, t3, rows, ps, valid, norms = take(9)
    norm_sums, norm_pair, norm_plane, norm_line = take(4)
    (psend, precv, gsend, grecv, hsend, hrecv, rsend, rrecv, bsend, brecv, nsend, nrecv, local) = refs
    at = Place()
    greet(at)
    layer = Layer(
        own_images=own_images,
        full_s=full_s,
        full_in=full_in,
        full_out=full_out,
        rows=rows,
        qkv=qkv,
        cq=cq,
        mkv=mkv,
        ps=ps,
        t2=t2,
        t3=t3,
        lengths=lengths,
        valid=valid,
        norms=norms,
        norm_grads=norm_sums,
        **dict(zip(NAMES, narrow)),
        **dict(zip(WIDE, wide)),
    )
    half, dmodel = full_s.shape[4:]
    lanes, half_in, lanes_out = dmodel // 2, full_in.shape[4], full_out.shape[5] // 2

    pairs = [pair_s.at[i] for i in range(8)] + [pair_in]
    own, other = [], []
    for i in range(9):
        depth = shards[i].shape[0]
        mine = pairs[i].at[pl.ds(pl.multiple_of(at.c * depth, 8), depth), :]
        other.append(remote(shards[i], mine, psend.at[i], precv.at[i], at.sib))
        own.append(pltpu.make_async_copy(shards[i], mine, local.at[i]))
    for core, peer in ((at.c, None), (at.oc, at.sib)):
        src = shards[9].at[pl.ds(pl.multiple_of(core * half, 16), half), :]
        if peer is None:
            own.append(pltpu.make_async_copy(src, pair_out.at[at.c], local.at[9]))
        else:
            other.append(remote(src, pair_out.at[at.c], psend.at[9], precv.at[9], peer))
    for a, b in zip(other, own):
        a.start()
        b.start()
    load = pltpu.make_async_copy(text_in, layer.io, local.at[10])
    load.start()

    def ready(i):
        own[i].wait()
        if i < 9:
            depth = shards[i].shape[0]
            theirs = pairs[i].at[pl.ds(pl.multiple_of(at.oc * depth, 8), depth), :]
        else:
            theirs = pair_out.at[at.oc]
        remote(theirs, theirs, psend.at[i], precv.at[i], at.sib).wait_recv()

    x_lanes = pl.ds(pl.multiple_of(at.x * lanes, 128), lanes)

    def lay_small(w):
        ready(w)
        block = dot_nt(pick(half, 2 * half, at.c * half), pair_s[w])
        full_s[w, at.z, at.y, at.c, :, x_lanes] = block.astype(BF)

    def lay_third(s, part):
        if part == 0:
            start = 2 * half_in * s + at.c * half_in
            block = dot_nt(pick(half_in, pair_in.shape[1], start), pair_in[...])
            full_in[s, at.z, at.y, at.c, :, x_lanes] = block.astype(BF)
            return
        for b in range(4):
            lo = pl.multiple_of(at.x * lanes_out + 128 * b, 128)
            cut = (b % 2) * (128 * THIRDS) + 128 * s
            full_out[s, at.z, at.y, at.c, :, pl.ds(lo, 128)] = pair_out[
                b // 2, :, cut : cut + 128
            ]

    g_small = [
        Gather(at, full_s, slice(*span), 128, gsend, grecv, g)
        for g, span in enumerate(SMALL)
    ]
    g_feed = []
    for s in range(THIRDS):
        index = len(SMALL) + 2 * s
        span = slice(s, s + 1)
        g_feed.append(
            (
                Gather(at, full_in, span, 128, gsend, grecv, index),
                Gather(at, full_out, span, 256, gsend, grecv, index + 1),
            )
        )

    def begin(group):
        for w in range(group.span.start, group.span.stop):
            lay_small(w)
        group.begin()

    arrived = []

    def begin_third(s, part):
        if part not in arrived:
            arrived.append(part)
            ready(8 + part)
        lay_third(s, part)
        g_feed[s][part].begin()

    here = pl.ds(pl.multiple_of(at.m * own_images, 8), own_images)
    keep = pltpu.make_async_copy(rows_in.at[:, here, :], rows.at[at.m], local.at[11])

    def begin_memory():
        for k in range(1, 8):
            to = lax.rem(at.m + k, 8) * own_images
            src = rows_in.at[:, pl.ds(pl.multiple_of(to, 8), own_images), :]
            remote(src, rows.at[at.m], rsend.at[0], rrecv.at[k - 1], at.mpeer(k)).start()
        keep.start()

    for i, vector in enumerate(vectors):
        norms[i : i + 1, :] = vector[...].reshape(1, dmodel)
    row = lax.broadcasted_iota(jnp.int32, valid.shape, 0)
    limit = jnp.zeros(valid.shape, jnp.int32)
    for i in range(own_images):
        first = i * layer.txt
        limit = jnp.where(row >= first, first + lengths[i], limit)
    valid[...] = jnp.where(row < limit, 1.0, 0.0).astype(BF)

    def each(groups, name):
        for group in groups:
            getattr(group, name)()

    seven = rows.at[pl.ds(0, 7)]

    def end_memory():
        keep.wait()
        for k in range(1, 8):
            ref = rows.at[lax.rem(at.m + 8 - k, 8)]
            remote(ref, ref, rsend.at[0], rrecv.at[k - 1], at.sib).wait_recv()

    def drain_small():
        for copy in other:
            copy.wait_send()
        remote(seven, seven, rsend.at[0], rrecv.at[0], at.sib).wait_send()
        each(g_small, "drain")

    def send_memory():
        for k in range(1, 8):
            src, dst = rows.at[lax.rem(at.m + k, 8)], rows_out.at[:, here, :]
            remote(src, dst, bsend.at[0], brecv.at[k - 1], at.mpeer(k)).start()
        keep_back.start()

    def move(src, dst, i):
        return pltpu.make_async_copy(src, dst, local.at[i])

    top, text = move(top_in, layer.io, 10), move(text_in, layer.sm, 10)
    away, again = move(ps, spill, 13), move(spill, ps, 13)
    packed = t3.at[:, 0:dmodel]
    save_out, save_text = move(packed, layer_out, 12), move(packed, text_out, 12)
    keep_back = move(rows.at[at.m], rows_out.at[:, here, :], 11)
    norm = NormSum(at, norm_sums, norm_pair, norm_plane, norm_line, norm_out, nsend, nrecv)
    fin_s, fin_in, fin_out = fins
    stores = []

    def store(group, out):
        group.last()
        copy = move(group.fin, out.at[group.span], 14 + len(stores))
        copy.start()
        stores.append(copy)

    r_feed, r_small = [], []
    for s in range(THIRDS):
        span = slice(s, s + 1)
        r_feed.append(
            [
                Reduce(at, full, span, bufs[2 * s + i], hsend, hrecv, 2 * s + i)
                for i, full in enumerate((full_in, full_out))
            ]
        )
    for g, span in enumerate(SMALL_BACK):
        n = 2 * THIRDS + g
        r_small.append(Reduce(at, full_s, slice(*span), bufs[n], hsend, hrecv, n))

    begin(g_small[1])
    begin(g_small[0])
    begin_third(1, 0)
    begin(g_small[2])
    g_small[0].second(1)
    begin(g_small[3])
    g_small[1].second(1)
    g_small[0].second(2)
    g_small[0].second(3)
    g_feed[1][0].second(1)
    begin(g_small[4])
    begin_third(0, 0)
    g_small[1].second(2)
    g_small[2].second(1)
    g_small[0].third(1)
    g_small[1].second(3)
    begin_third(1, 1)
    g_small[2].second(2)
    g_small[3].second(1)
    g_small[1].third(0)
    g_small[2].second(3)
    load.wait()
    layer.norm_into(layer.io, 0)
    g_small[1].third(1)
    g_small[3].second(2)
    g_small[0].third(0)
    g_small[2].third(0)
    g_small[3].second(3)
    begin_memory()
    g_feed[1][0].second(2)
    g_small[0].fourth()
    g_small[1].fourth()
    g_small[4].second(1)
    g_small[0].last()
    g_small[3].third(0)
    g_feed[1][0].second(3)
    g_small[3].third(1)
    begin_third(0, 1)
    g_small[1].last()
    g_feed[0][0].second(1)
    g_small[4].second(2)
    g_small[4].second(3)
    g_feed[0][0].second(2)
    g_feed[1][1].second(1)
    g_feed[0][0].second(3)
    g_feed[1][1].second(2)
    g_small[2].third(1)
    g_feed[1][1].second(3)
    layer.project(layer.qkv, lambda: layer.nrm[...], 0)
    layer.self_forward(0, 2)
    layer.self_forward(2, 4)
    away.start()
    g_feed[0][0].third(1)
    g_small[4].third(0)
    g_feed[1][0].third(1)
    begin_third(2, 0)
    g_small[3].fourth()
    g_small[2].fourth()
    g_feed[0][0].third(0)
    g_small[2].last()
    g_feed[1][1].third(1)
    g_feed[1][0].third(0)
    layer.add_after_self()
    top.start()
    g_small[4].third(1)
    g_feed[1][1].third(0)
    layer.norm_into(layer.after_self, 1)
    layer.project(layer.cq, lambda: layer.nrm[...], 4)
    begin_third(2, 1)
    g_small[3].last()
    g_feed[0][0].fourth()
    g_feed[0][0].last()
    g_feed[1][0].fourth()
    end_memory()
    layer.memory_in()
    g_feed[0][1].second(1)
    layer.project(layer.mkv, layer.memory, 5)
    g_feed[0][1].second(2)
    g_feed[0][1].second(3)
    g_feed[1][1].fourth()
    g_small[4].fourth()
    away.wait()
    layer.cross_forward(0, 4)
    g_feed[0][1].third(0)
    g_feed[0][1].third(1)
    g_feed[2][0].second(1)
    layer.cross_forward(4, 8)
    g_feed[2][0].second(2)
    g_feed[1][1].last()
    g_small[4].last()
    g_feed[2][1].second(1)
    g_feed[2][1].second(2)
    layer.add_after_cross()
    g_feed[0][1].fourth()
    layer.norm_into(layer.after_cross, 2)
    top.wait()
    layer.mask_top()
    layer.feed_start()
    drain_small()
    g_feed[2][1].second(3)
    g_feed[0][1].last()
    g_feed[2][0].second(3)
    each(g_feed[0], "drain")
    layer.feed_chunk(0)
    g_feed[2][1].third(1)
    r_feed[0][0].begin()
    g_feed[2][1].third(0)
    g_feed[2][0].third(0)
    g_feed[1][0].last()
    r_feed[0][1].begin()
    g_feed[2][0].third(1)
    each(g_feed[1], "drain")
    layer.feed_chunk(1)
    r_feed[0][0].second()
    g_feed[2][1].fourth()
    g_feed[2][0].fourth()
    r_feed[0][1].second()
    g_feed[2][0].last()
    r_feed[1][0].begin()
    g_feed[2][1].last()
    r_feed[0][0].third(0)
    each(g_feed[2], "drain")
    layer.feed_chunk(2)
    r_feed[0][1].third(1)
    r_feed[2][0].begin()
    r_feed[0][1].third(0)
    layer.third_back()
    r_feed[1][0].second()
    r_feed[0][0].third(1)
    layer.output_back(7, layer.cm, t2)
    r_feed[2][0].second()
    layer.cross_back(0, 4)
    r_feed[1][0].third(0)
    r_feed[1][1].begin()
    r_feed[1][0].third(1)
    r_feed[0][1].fourth()
    layer.cross_back(4, 8)
    again.start()
    r_feed[0][0].fourth()
    r_feed[2][0].third(1)
    r_feed[2][1].begin()
    r_small[0].begin()
    r_feed[2][0].third(0)
    layer.layer_out(t3)
    save_out.start()
    layer.memory_back()
    r_feed[1][0].fourth()
    r_feed[1][1].second()
    layer.second_up()
    r_small[0].second()
    layer.weight_grads(layer.mkv, layer.memory, 5)
    r_feed[2][0].fourth()
    r_feed[2][1].second()
    r_small[4].begin()
    layer.memory_out()
    r_small[0].third(0)
    r_small[0].third(1)
    send_memory()
    layer.norm_into(layer.after_self, 1)
    layer.weight_grads(layer.cq, lambda: layer.nrm[...], 4)
    r_feed[1][1].third(0)
    r_small[1].begin()
    layer.second_back()
    r_small[4].second()
    r_feed[1][1].third(1)
    r_feed[0][1].fifth()
    layer.output_back(3, layer.sm, t2)
    text.start()
    text.wait()
    layer.norm_into(layer.sm, 0)
    again.wait()
    layer.self_back(0, 2)
    r_small[1].second()
    layer.self_back(2, 4)
    r_small[4].third(0)
    layer.first_up()
    layer.weight_grads(layer.qkv, lambda: layer.nrm[...], 0)
    r_small[4].third(1)
    r_feed[2][1].third(0)
    r_small[1].third(1)
    r_feed[1][0].fifth()
    r_small[3].begin()
    r_small[0].fourth()
    r_feed[0][0].fifth()
    r_small[1].third(0)
    r_small[2].begin()
    store(r_feed[1][0], fin_in)
    r_feed[2][1].third(1)
    r_small[2].second()
    store(r_feed[0][1], fin_out)
    save_out.wait()
    layer.first_back(layer.sm, t3)
    save_text.start()
    r_feed[2][0].fifth()
    r_small[4].fourth()
    r_feed[1][1].fourth()
    r_small[3].second()
    r_small[2].third(0)
    r_small[2].third(1)
    r_small[3].third(0)
    r_small[1].fourth()
    norm.start(0)
    r_feed[2][1].fourth()
    r_small[3].third(1)
    r_small[2].fourth()
    r_feed[1][1].fifth()
    r_small[0].fifth()
    store(r_feed[2][0], fin_in)
    r_small[4].fifth()
    store(r_small[0], fin_s)
    r_small[3].fourth()
    r_small[1].fifth()
    norm.finish(0)
    norm.start(1)
    r_small[2].fifth()
    norm.finish(1)
    norm.start(2)
    store(r_feed[1][1], fin_out)
    r_feed[2][1].fifth()
    r_small[3].fifth()
    store(r_feed[0][0], fin_in)
    store(r_small[4], fin_s)
    store(r_small[2], fin_s)
    store(r_small[1], fin_s)
    store(r_small[3], fin_s)
    store(r_feed[2][1], fin_out)
    norm.finish(2)

    save_text.wait()
    keep_back.wait()
    for k in range(1, 8):
        m = lax.rem(at.m + 8 - k, 8)
        there = pl.ds(pl.multiple_of(m * own_images, 8), own_images)
        ref = rows_out.at[:, there, :]
        remote(ref, ref, bsend.at[0], brecv.at[k - 1], at.sib).wait_recv()
    remote(seven, seven, bsend.at[0], brecv.at[0], at.sib).wait_send()
    for copy in norm.out:
        copy.wait_send()
    each(r_small, "drain")
    for groups in r_feed:
        each(groups, "drain")
    for copy in stores:
        copy.wait()


def whole(shards, rows, text, top, lengths, vectors):
    depth, width = shards[0].shape
    dmodel = depth * 4
    half = width // 2
    lanes = dmodel // 2
    ff = shards[8].shape[1] * 8
    units = ff // THIRDS
    half_in = units // 16
    shapes = [
        (8, 4, 2, 2, half, dmodel),
        (THIRDS, 4, 2, 2, half_in, dmodel),
        (THIRDS, 4, 2, 2, half, units),
    ]
    tokens = text.shape[0]
    images = lengths.shape[0]
    mem_rows = rows.shape[0] * rows.shape[1]
    groups = dmodel // 256
    any_ = pl.BlockSpec(memory_space=pl.ANY)
    vmem = pl.BlockSpec(memory_space=pltpu.VMEM)
    smem = pl.BlockSpec(memory_space=pltpu.SMEM)
    sems = pltpu.SemaphoreType.DMA
    scratch = [pltpu.VMEM(s, BF) for s in shapes]
    scratch += [
        pltpu.VMEM((8, 2 * depth, width), BF),
        pltpu.VMEM((2 * depth, 4 * width), BF),
        pltpu.VMEM((2, half, 4 * depth), BF),
    ]
    for _ in range(THIRDS):
        scratch += reduce_bufs(1, half_in, lanes, 128)
        scratch += reduce_bufs(1, half, units // 2, 256)
    for a, b in SMALL_BACK:
        scratch += reduce_bufs(b - a, half, lanes, 128)
    scratch += [pltpu.VMEM((tokens, dmodel), BF) for _ in NAMES]
    scratch += [pltpu.VMEM((tokens, dmodel), F32) for _ in WIDE]
    stacks = [(3, tokens, dmodel), (1, tokens, dmodel), (2, mem_rows, dmodel)]
    scratch += [pltpu.VMEM(s, BF) for s in stacks]
    scratch += [
        pltpu.VMEM((tokens, units), BF),
        pltpu.VMEM((tokens, units), BF),
        pltpu.VMEM((8, rows.shape[0], images, dmodel), BF),
        pltpu.VMEM((images // 2, groups, 512, 128), BF),
        pltpu.VMEM((tokens, 128), BF),
        pltpu.VMEM((8, dmodel), F32),
        pltpu.VMEM((8, dmodel), F32),
        pltpu.VMEM((8, dmodel), F32),
        pltpu.VMEM((4, 8, dmodel), F32),
        pltpu.VMEM((4, 8, dmodel), F32),
    ]
    gathers = len(SMALL) + 2 * THIRDS
    reduces = len(SMALL_BACK) + 2 * THIRDS
    counts = (10, 10, Gather.SENDS * gathers, Gather.RECVS * gathers)
    counts += (reduces, Reduce.RECVS * reduces, 1, 7, 1, 7, 7, 7, 14 + reduces)
    scratch += [sems((n,)) for n in counts]
    return pl.pallas_call(
        functools.partial(whole_kernel, images),
        out_shape=[
            jax.ShapeDtypeStruct((8, 2, half, lanes), BF),
            jax.ShapeDtypeStruct((THIRDS, 2, half_in, lanes), BF),
            jax.ShapeDtypeStruct((THIRDS, 2, half, units // 2), BF),
            jax.ShapeDtypeStruct(text.shape, BF),
            jax.ShapeDtypeStruct(text.shape, BF),
            jax.ShapeDtypeStruct(rows.shape, BF),
            jax.ShapeDtypeStruct((8, dmodel), F32),
            jax.ShapeDtypeStruct((images // 2, groups, 512, 128), BF),
        ],
        in_specs=[any_] * 13 + [smem] + [vmem] * 6,
        out_specs=[any_] * 6 + [vmem, any_],
        scratch_shapes=scratch,
        compiler_params=pltpu.CompilerParams(
            collective_id=0, has_side_effects=True, vmem_limit_bytes=63 << 20
        ),
    )(*shards, rows, text, top, lengths, *vectors)


def finish_kernel(*refs):
    fin_s, fin_in, fin_out, norm, *moved = refs[:7]
    outs, norm_outs, targets, sem = refs[7:17], refs[17:23], refs[23:26], refs[26]
    copies = []
    for i, (a, b) in enumerate(zip(moved, targets)):
        copy = pltpu.make_async_copy(a, b, sem.at[i])
        copy.start()
        copies.append(copy)
    c = lax.rem(lax.axis_index("dp"), 2)
    depth = outs[0].shape[0]
    sel = pick(depth, 2 * depth, c * depth)
    for w in range(8):
        both = fin_s[w].reshape(outs[w].shape[1], 2 * depth)
        outs[w][...] = dot_nt(sel, both)
    outs[8][...] = dot_nt(sel, fin_in[...].reshape(outs[8].shape[1], 2 * depth))
    half = fin_out.shape[2]
    for s in range(THIRDS):
        for h in range(2):
            for b in range(2):
                lo = pl.multiple_of(c * 256 + 128 * b, 128)
                cut = b * (128 * THIRDS) + 128 * s
                outs[9][half * h : half * (h + 1), cut : cut + 128] = fin_out[
                    s, h, :, pl.ds(lo, 128)
                ].astype(F32)
    for i, out in enumerate(norm_outs):
        out[...] = norm[i : i + 1, :].reshape(out.shape)
    for copy in copies:
        copy.wait()


def finish(fin_s, fin_in, fin_out, norm, moved, shapes):
    any_ = pl.BlockSpec(memory_space=pl.ANY)
    vmem = pl.BlockSpec(memory_space=pltpu.VMEM)
    return pl.pallas_call(
        finish_kernel,
        out_shape=[jax.ShapeDtypeStruct(s, F32) for s in shapes]
        + [jax.ShapeDtypeStruct(norm.shape[1:], F32)] * 6
        + [jax.ShapeDtypeStruct(a.shape, a.dtype) for a in moved],
        in_specs=[vmem] * 7,
        out_specs=[vmem] * 16 + [any_] * 3,
        scratch_shapes=[pltpu.SemaphoreType.DMA((3,))],
    )(fin_s, fin_in, fin_out, norm, *moved)


def fits(mesh_shape, text, memory, mats):
    images, txt, dmodel = text.shape
    depth, width = mats[0].shape
    return (
        mesh_shape["dp"] == 4
        and mesh_shape["mem"] == 8
        and images == 8
        and txt == HEAD == 64
        and memory.shape[0] == 8 * images
        and (memory.shape[1] * 8) % 32 == 0
        and memory.shape[1] * 8 <= 128
        and dmodel == HEADS * HEAD == 4 * depth == 8 * width
        and dmodel % 256 == 0
        and width % 32 == 0
        and mats[8].shape == (depth, 4 * width)
        and 4 * width == 128 * THIRDS
        and mats[9].shape == (4 * depth, width)
    )


def shards_lean(text, lengths, memory, out_grad, *params):
    mats, vectors = params[:10], params[10:]
    images, txt, dmodel = text.shape
    tokens = images * txt
    mats = mats[:9] + (mats[9].T,)
    fin_s, fin_in, fin_out, layer_out, text_grad, back, norm_sums, _ = whole(
        mats,
        memory.transpose(1, 0, 2),
        text.reshape(tokens, dmodel),
        out_grad.reshape(tokens, dmodel),
        lengths,
        vectors,
    )
    *grads, layer_out, text_grad, back = finish(
        fin_s,
        fin_in,
        fin_out,
        norm_sums,
        (layer_out, text_grad, back),
        [mat.shape for mat in mats],
    )
    return (
        layer_out.reshape(text.shape),
        text_grad.reshape(text.shape),
        back.transpose(1, 0, 2),
        *grads[:9],
        grads[9].T,
        *grads[10:],
    )


def solution(mesh):
    def pick_form(text, lengths, memory, out_grad, *params):
        lean = fits(mesh.shape, text, memory, params[:10])
        form = shards_lean if lean else shards
        return form(text, lengths, memory, out_grad, *params)

    return jax.shard_map(
        pick_form,
        mesh=mesh,
        in_specs=(
            P(("dp", "mem"), None, None),
            P(("dp", "mem")),
            P("dp", "mem", None),
            P(("dp", "mem"), None, None),
            P("dp", "mem"),
            P("dp", "mem"),
            P("dp", "mem"),
            P("dp", "mem"),
            P("dp", "mem"),
            P("dp", "mem"),
            P("dp", "mem"),
            P("dp", "mem"),
            P("dp", "mem"),
            P("dp", "mem"),
            P(),
            P(),
            P(),
            P(),
            P(),
            P(),
        ),
        out_specs=(
            P(("dp", "mem"), None, None),
            P(("dp", "mem"), None, None),
            P("dp", "mem", None),
            P("dp", "mem"),
            P("dp", "mem"),
            P("dp", "mem"),
            P("dp", "mem"),
            P("dp", "mem"),
            P("dp", "mem"),
            P("dp", "mem"),
            P("dp", "mem"),
            P("dp", "mem"),
            P("dp", "mem"),
            P(),
            P(),
            P(),
            P(),
            P(),
            P(),
        ),
        check_vma=False,
    )
```

profile of v0, /device:TPU:0, one launch (start us, length us, event | category | flops | bytes accessed | tf_op | source)
XLA Modules:
  0.0 226.1 jit_solution(1165848057175004322)
XLA Ops:
  0.7 220.5 %shard_map.339 = (bf16[8,2,48,384]{3,2,1,0:T(8,128)(2,1)}, bf16[3,2,64,384]{3,2,1,0:T(8,128)(2,1)}, bf16[3,2,48,512]{3,2,1,0:T(8,128)(2,1)}, bf16[512,768]{1,0:T...) custom-call(bf16[192,96]{1,0:T(8,128)(2,1)} %refs_0_.1, ...), custom_call_target="tpu_custom_call" | custom-call | tf_op jit(solution)/shard_map/pallas_call | solution.py:1501
  221.1 4.8 %shard_map.340 = (f32[192,96]{1,0:T(8,128)}, f32[192,96]{1,0:T(8,128)}, f32[192,96]{1,0:T(8,128)}, f32[192,96]{1,0:T(8,128)}, f32[192,96]{1,0:T(8,128)}, /*index...) custom-call(bf16[8,2,48,384]{3,2,1,0:T(8,128)(2,1)} %get-tuple-eleme, ...), custom_call_target="tpu_custom_call" | custom-call | tf_op jit(solution)/shard_map/pallas_call | solution.py:1555
where the time goes:
time: 227 us; the launch traced here: 226 us
  Pallas kernels  225 us (99%)
    pallas_call x1, Pallas kernels, whole(): pl.pallas_call(functools.partial(whole_kernel, images), out_shape=[jax.Sh...  220 us
    pallas_call x1, Pallas kernels, finish(): pl.pallas_call(finish_kernel, out_shape=[jax.ShapeDtypeStruct(s, F32) for...  4.79 us

commit v1 on v0

--- a/solution.py
+++ b/solution.py
@@ -366,11 +366,15 @@
         self.yn = (self.d, self.z * 2 + self.oy)
         self.xyn = (self.ox * 2 + self.c, self.z * 2 + self.oy)
 
-    def zup(self, k):
-        return lax.rem(self.z + k, 4)
+        self.side = lax.div(self.z, 2)
+        self.inner = lax.rem(lax.div(self.z + 1, 2), 2) == 1
+        self.flip = self.z + 1 - 2 * lax.rem(self.z, 2)
+        self.ours, self.theirs = pl.ds(2 * self.side, 2), pl.ds(2 - 2 * self.side, 2)
+        self.flip_peer = (self.d, self.flip * 2 + self.y)
+        self.across = (self.d, (3 - self.z) * 2 + self.y)
 
     def zpeer(self, k):
-        return (self.d, self.zup(k) * 2 + self.y)
+        return (self.d, lax.rem(self.z + k, 4) * 2 + self.y)
 
     def mpeer(self, k):
         return (self.d, lax.rem(self.m + k, 8))
@@ -396,7 +400,7 @@
 
 
 class Gather:
-    SENDS, RECVS = 3, 8
+    SENDS, RECVS = 4, 7
 
     def __init__(self, at, full, span, via_y, sends, recvs, index):
         self.at, self.full, self.span = at, full, span
@@ -416,70 +420,134 @@
     def got(self, slot, ref):
         remote(ref, ref, self.sends[0], self.recvs[slot], self.at.sib).wait_recv()
 
+    def sent(self, kind, ref):
+        remote(ref, ref, self.sends[kind], self.recvs[0], self.at.sib).wait_send()
+
+    def line(self, z):
+        return self.piece(z, self.at.y, self.at.c, self.at.x)
+
     def begin(self):
         at = self.at
-        own = self.piece(at.z, at.y, at.c, at.x)
-        for k in (1, 2, 3):
-            self.send(2, k - 1, own, at.zpeer(k))
-        self.send(1, 3, own, at.xn)
-        self.send(1, 4, own, at.yn)
-        self.send(0, 7, own, at.sib)
+        own = self.line(at.z)
+        self.send(2, 0, own, at.flip_peer)
+        self.send(1, 2, own, at.xn)
+        self.send(1, 3, own, at.yn)
+        self.send(0, 6, own, at.sib)
+
+    def spread(self, ref):
+        at = self.at
+        self.send(1, 2, ref, at.xn)
+        self.send(1, 3, ref, at.yn)
+        self.send(0, 6, ref, at.sib)
 
     def second(self, k):
         at = self.at
-        ref = self.piece(at.zup(4 - k), at.y, at.c, at.x)
-        self.got(k - 1, ref)
-        self.send(1, 3, ref, at.xn)
-        self.send(1, 4, ref, at.yn)
-        self.send(0, 7, ref, at.sib)
+        if k == 1:
+            self.got(0, self.line(at.flip))
+            pl.when(at.inner)(lambda: self.send(3, 1, self.line(at.ours), at.across))
+            self.spread(self.line(at.flip))
+        elif k == 2:
+
+            @pl.when(at.inner)
+            def _():
+                self.got(1, self.line(at.theirs))
+                self.send(3, 1, self.line(at.theirs), at.flip_peer)
+        else:
+            pl.when(~at.inner)(lambda: self.got(1, self.line(at.theirs)))
+            self.spread(self.line(at.theirs))
 
     def third(self, part):
         at, every = self.at, slice(None)
         x, y, peer = ((at.ox, at.y, at.yn), (at.x, at.oy, at.xn))[part]
         ref = self.piece(every, y, at.c, x)
-        self.got(3 + part, ref)
-        self.send(1, 5 + part, self.piece(every, y, at.c, x, self.cuts[part]), peer)
-        self.send(0, 7, ref, at.sib)
+        self.got(2 + part, ref)
+        self.send(1, 4 + part, self.piece(every, y, at.c, x, self.cuts[part]), peer)
+        self.send(0, 6, ref, at.sib)
 
     def fourth(self):
         at = self.at
         for part, cut in enumerate(self.cuts):
             ref = self.piece(slice(None), at.oy, at.c, at.ox, cut)
-            self.got(5 + part, ref)
-            self.send(0, 7, ref, at.sib)
+            self.got(4 + part, ref)
+            self.send(0, 6, ref, at.sib)
 
     def last(self):
-        self.got(7, self.full.at[self.span, :, :, self.at.oc])
+        self.got(6, self.full.at[self.span, :, :, self.at.oc])
 
     def drain(self):
         at = self.at
-        for kind, ref in enumerate(
-            (
-                self.full.at[self.span, :, :, at.c],
-                self.full.at[self.span, pl.ds(0, 3), :, at.c],
-                self.piece(pl.ds(0, 3), at.y, at.c, at.x),
-            )
-        ):
-            remote(ref, ref, self.sends[kind], self.recvs[0], at.sib).wait_send()
+        self.sent(0, self.full.at[self.span, :, :, at.c])
+        self.sent(1, self.full.at[self.span, pl.ds(0, 3), :, at.c])
+        self.sent(2, self.line(at.z))
+        pl.when(at.inner)(lambda: self.sent(3, self.line(slice(None))))
+
+
+class GatherLast(Gather):
+    def block(self, z):
+        return self.full.at[self.span, z, :, self.at.c]
+
+    def begin(self):
+        self.spread(self.line(self.at.z))
+
+    def third(self, part):
+        at = self.at
+        x, y, peer = ((at.ox, at.y, at.yn), (at.x, at.oy, at.xn))[part]
+        ref = self.piece(at.z, y, at.c, x)
+        self.got(2 + part, ref)
+        self.send(1, 4 + part, self.piece(at.z, y, at.c, x, self.cuts[part]), peer)
+        self.send(0, 6, ref, at.sib)
+
+    def fourth(self):
+        at = self.at
+        for part, cut in enumerate(self.cuts):
+            ref = self.piece(at.z, at.oy, at.c, at.ox, cut)
+            self.got(4 + part, ref)
+            self.send(0, 6, ref, at.sib)
+        self.send(2, 0, self.block(at.z), at.flip_peer)
+
+    def second(self, k):
+        at = self.at
+        if k == 1:
+            ref = self.block(at.flip)
+            self.got(0, ref)
+            pl.when(at.inner)(lambda: self.send(3, 1, self.block(at.ours), at.across))
+            self.send(0, 6, ref, at.sib)
+        elif k == 2:
+
+            @pl.when(at.inner)
+            def _():
+                self.got(1, self.block(at.theirs))
+                self.send(3, 1, self.block(at.theirs), at.flip_peer)
+        else:
+            pl.when(~at.inner)(lambda: self.got(1, self.block(at.theirs)))
+            self.send(0, 6, self.block(at.theirs), at.sib)
+
+    def drain(self):
+        at = self.at
+        self.sent(0, self.full.at[self.span, :, :, at.c])
+        self.sent(1, self.line(pl.ds(0, 3)))
+        self.sent(2, self.block(at.z))
+        pl.when(at.inner)(lambda: self.sent(3, self.full.at[self.span, :, :, at.c]))
 
 
 class Reduce:
-    RECVS = 7
+    RECVS = 9
 
     def __init__(self, at, full, span, bufs, sends, recvs, index):
         self.at, self.full, self.span = at, full, span
-        self.chip, self.via_y, self.via_x, self.rx, self.ry, self.rz, self.fin = bufs
-        self.sent = sends.at[index]
+        (self.chip, self.via_y, self.via_x, self.rx, self.ry) = bufs[:5]
+        (self.outer, self.middle, self.pair, self.fin) = bufs[5:]
+        self.sends = sends.at[index]
         self.recvs = [recvs.at[self.RECVS * index + i] for i in range(self.RECVS)]
         self.count, self.lanes = self.chip.shape[0], full.shape[-1] // 2
         cut = self.via_y.shape[-1]
         self.cuts = (slice(0, cut), slice(cut, self.lanes))
 
     def send(self, slot, src, dst, peer):
-        remote(src, dst, self.sent, self.recvs[slot], peer).start()
+        remote(src, dst, self.sends, self.recvs[slot], peer).start()
 
     def got(self, slot, ref):
-        remote(ref, ref, self.sent, self.recvs[slot], self.at.sib).wait_recv()
+        remote(ref, ref, self.sends, self.recvs[slot], self.at.sib).wait_recv()
 
     def begin(self):
         at = self.at
@@ -488,7 +556,7 @@
             src = self.full.at[self.span, :, :, at.oc, :, lanes]
             self.send(0, src, self.chip.at[:, x], at.sib)
 
-    def second(self):
+    def add_cores(self):
         at = self.at
         chip, full, lanes, w0 = self.chip, self.full, self.lanes, self.span.start
         self.got(0, chip)
@@ -504,6 +572,10 @@
             return carry
 
         lax.fori_loop(0, 8 * self.count, add, 0)
+
+    def second(self):
+        at, chip = self.at, self.chip
+        self.add_cores()
         self.send(1, chip.at[:, at.ox, :, at.oy, :, self.cuts[0]], self.via_y, at.yn)
         self.send(2, chip.at[:, at.ox, :, at.oy, :, self.cuts[1]], self.via_x, at.xn)
 
@@ -540,43 +612,144 @@
             return carry
 
         lax.fori_loop(0, 4 * self.count, add, 0)
-        for k in (1, 2, 3):
-            src = chip.at[:, at.x, at.zup(k), at.y]
-            self.send(5, src, self.rz.at[k - 1], at.zpeer(k))
-
-    def fifth(self):
+        self.inward()
+
+    def line(self, z):
+        return self.chip.at[:, self.at.x, z, self.at.y]
+
+    def inward(self):
         at = self.at
-        self.got(5, self.rz)
+        pl.when(~at.inner)(
+            lambda: self.send(5, self.line(at.theirs), self.outer, at.flip_peer)
+        )
+
+    def add_line(self, start, ref):
+        at, chip = self.at, self.chip
+
+        def add(i, carry):
+            w, z = lax.div(i, 2), lax.rem(i, 2)
+            chip[w, at.x, start + z, at.y] = (
+                chip[w, at.x, start + z, at.y].astype(F32) + ref[w, z].astype(F32)
+            ).astype(BF)
+            return carry
+
+        lax.fori_loop(0, 2 * self.count, add, 0)
+
+    def relay(self, stage):
+        at = self.at
+        if stage == 0:
+
+            @pl.when(at.inner)
+            def _():
+                self.got(5, self.outer)
+                self.add_line(2 - 2 * at.side, self.outer)
+                self.send(6, self.line(at.theirs), self.middle, at.across)
+
+            return
+
+        @pl.when(at.inner)
+        def _():
+            self.got(6, self.middle)
+            self.add_line(2 * at.side, self.middle)
+
+        self.send(7, self.line(at.flip), self.pair, at.flip_peer)
+
+    def finish(self, terms):
+        at = self.at
 
         def add(w, carry):
             total = self.chip[w, at.x, at.z, at.y].astype(F32)
-            for k in range(3):
-                total = total + self.rz[k, w].astype(F32)
+            for term in terms:
+                total = total + term[w].astype(F32)
             self.fin[w, at.c] = total.astype(BF)
             return carry
 
         lax.fori_loop(0, self.count, add, 0)
         mine = self.fin.at[:, at.c]
-        self.send(6, mine, mine, at.sib)
+        self.send(8, mine, mine, at.sib)
+
+    def fifth(self):
+        self.got(7, self.pair)
+        self.finish([self.pair])
 
     def last(self):
-        self.got(6, self.fin.at[:, self.at.oc])
+        self.got(8, self.fin.at[:, self.at.oc])
 
     def drain(self):
         ref = self.full.at[self.span]
-        remote(ref, ref, self.sent, self.recvs[0], self.at.sib).wait_send()
-
-
-def reduce_bufs(count, rows, lanes, cut):
-    return [
-        pltpu.VMEM((count, 2, 4, 2, rows, lanes), BF),
-        pltpu.VMEM((count, 4, rows, cut), BF),
-        pltpu.VMEM((count, 4, rows, lanes - cut), BF),
-        pltpu.VMEM((count, 4, rows, lanes), BF),
-        pltpu.VMEM((count, 4, rows, lanes), BF),
-        pltpu.VMEM((3, count, rows, lanes), BF),
-        pltpu.VMEM((count, 2, rows, lanes), BF),
-    ]
+        remote(ref, ref, self.sends, self.recvs[0], self.at.sib).wait_send()
+
+
+class ReduceFirst(Reduce):
+    def line(self, z):
+        return self.chip.at[:, :, z]
+
+    def second(self):
+        self.add_cores()
+        self.inward()
+
+    def add_line(self, start, ref, n=2):
+        chip = self.chip
+
+        def add(i, carry):
+            w, r = lax.div(i, 4 * n), lax.rem(i, 4 * n)
+            z, r = lax.div(r, 4), lax.rem(r, 4)
+            x, y = lax.div(r, 2), lax.rem(r, 2)
+            chip[w, x, start + z, y] = (
+                chip[w, x, start + z, y].astype(F32) + ref[w, x, z, y].astype(F32)
+            ).astype(BF)
+            return carry
+
+        lax.fori_loop(0, 4 * n * self.count, add, 0)
+
+    def fourth(self):
+        at, chip = self.at, self.chip
+        self.got(7, self.pair)
+
+        def add(i, carry):
+            w, r = lax.div(i, 4), lax.rem(i, 4)
+            x, y = lax.div(r, 2), lax.rem(r, 2)
+            chip[w, x, at.z, y] = (
+                chip[w, x, at.z, y].astype(F32) + self.pair[w, x, y].astype(F32)
+            ).astype(BF)
+            return carry
+
+        lax.fori_loop(0, 4 * self.count, add, 0)
+        self.send(1, chip.at[:, at.ox, at.z, at.oy, :, self.cuts[0]], self.via_y, at.yn)
+        self.send(2, chip.at[:, at.ox, at.z, at.oy, :, self.cuts[1]], self.via_x, at.xn)
+
+    def third(self, part):
+        at, chip = self.at, self.chip
+        ref = (self.via_y, self.via_x)[part]
+        x, y = ((at.ox, at.y), (at.x, at.oy))[part]
+        cut = self.cuts[part]
+        self.got(1 + part, ref)
+
+        def add(w, carry):
+            chip[w, x, at.z, y, :, cut] = (
+                chip[w, x, at.z, y, :, cut].astype(F32) + ref[w].astype(F32)
+            ).astype(BF)
+            return carry
+
+        lax.fori_loop(0, self.count, add, 0)
+        box, peer = ((self.rx, at.xn), (self.ry, at.yn))[part]
+        self.send(3 + part, chip.at[:, x, at.z, y], box, peer)
+
+    def fifth(self):
+        self.got(3, self.rx)
+        self.got(4, self.ry)
+        self.finish([self.rx, self.ry])
+
+
+def reduce_bufs(count, rows, lanes, cut, z_first):
+    one, line, block = (rows, lanes), (4, rows, lanes), (2, 2, 2, rows, lanes)
+    if z_first:
+        shapes = [(rows, cut), (rows, lanes - cut), one, one, block, block, block[1:]]
+    else:
+        pair = (2, rows, lanes)
+        shapes = [(4, rows, cut), (4, rows, lanes - cut), line, line, pair, pair, one]
+    shapes = [(2, 4, 2, rows, lanes)] + shapes + [(2, rows, lanes)]
+    return [pltpu.VMEM((count,) + shape, BF) for shape in shapes]
 
 
 def pick(rows, cols, start):
@@ -1005,6 +1178,8 @@
 SMALL = ((0, 2), (2, 3), (3, 5), (5, 7), (7, 8))
 SMALL_BACK = ((7, 8), (4, 5), (3, 4), (0, 3), (5, 7))
 THIRDS = 3
+Z_LAST = (4, 9)
+Z_FIRST_BACK = (0, 6)
 NAMES = ("nrm", "io", "sm", "cm")
 WIDE = ("after_self", "after_cross", "acc_out", "acc_up")
 
@@ -1020,7 +1195,7 @@
     shards, (rows_in, text_in, top_in, lengths), vectors = take(10), take(4), take(6)
     fins, (layer_out, text_out, rows_out, norm_out, spill) = take(3), take(5)
     full_s, full_in, full_out, pair_s, pair_in, pair_out = take(6)
-    bufs = [take(7) for _ in range(2 * THIRDS + len(SMALL_BACK))]
+    bufs = [take(9) for _ in range(2 * THIRDS + len(SMALL_BACK))]
     narrow, wide = take(len(NAMES)), take(len(WIDE))
     qkv, cq, mkv, t2, t3, rows, ps, valid, norms = take(9)
     norm_sums, norm_pair, norm_plane, norm_line = take(4)
@@ -1097,8 +1272,12 @@
                 b // 2, :, cut : cut + 128
             ]
 
+    def gather(full, span, via_y, n):
+        form = GatherLast if n in Z_LAST else Gather
+        return form(at, full, span, via_y, gsend, grecv, n)
+
     g_small = [
-        Gather(at, full_s, slice(*span), 128, gsend, grecv, g)
+        gather(full_s, slice(*span), 128, g)
         for g, span in enumerate(SMALL)
     ]
     g_feed = []
@@ -1107,8 +1286,8 @@
         span = slice(s, s + 1)
         g_feed.append(
             (
-                Gather(at, full_in, span, 128, gsend, grecv, index),
-                Gather(at, full_out, span, 256, gsend, grecv, index + 1),
+                gather(full_in, span, 128, index),
+                gather(full_out, span, 256, index + 1),
             )
         )
 
@@ -1187,247 +1366,272 @@
         copy.start()
         stores.append(copy)
 
+    def reduce(full, span, n):
+        form = ReduceFirst if n in Z_FIRST_BACK else Reduce
+        return form(at, full, span, bufs[n], hsend, hrecv, n)
+
     r_feed, r_small = [], []
     for s in range(THIRDS):
         span = slice(s, s + 1)
         r_feed.append(
             [
-                Reduce(at, full, span, bufs[2 * s + i], hsend, hrecv, 2 * s + i)
+                reduce(full, span, 2 * s + i)
                 for i, full in enumerate((full_in, full_out))
             ]
         )
     for g, span in enumerate(SMALL_BACK):
         n = 2 * THIRDS + g
-        r_small.append(Reduce(at, full_s, slice(*span), bufs[n], hsend, hrecv, n))
+        r_small.append(reduce(full_s, slice(*span), n))
 
     begin(g_small[1])
+    begin(g_small[2])
+    begin_third(0, 1)
     begin(g_small[0])
-    begin_third(1, 0)
-    begin(g_small[2])
-    g_small[0].second(1)
-    begin(g_small[3])
     g_small[1].second(1)
-    g_small[0].second(2)
-    g_small[0].second(3)
-    g_feed[1][0].second(1)
+    begin_third(2, 1)
+    begin_third(2, 0)
     begin(g_small[4])
     begin_third(0, 0)
+    g_small[2].second(1)
+    begin(g_small[3])
+    g_small[0].second(1)
     g_small[1].second(2)
-    g_small[2].second(1)
-    g_small[0].third(1)
-    g_small[1].second(3)
-    begin_third(1, 1)
     g_small[2].second(2)
     g_small[3].second(1)
-    g_small[1].third(0)
-    g_small[2].second(3)
+    g_small[4].third(0)
     load.wait()
     layer.norm_into(layer.io, 0)
-    g_small[1].third(1)
+    g_small[4].third(1)
+    g_small[0].second(2)
+    g_feed[2][1].second(1)
+    g_small[1].second(3)
+    g_feed[0][0].second(1)
+    g_feed[0][1].second(1)
+    begin_third(1, 0)
+    begin_third(1, 1)
     g_small[3].second(2)
-    g_small[0].third(0)
-    g_small[2].third(0)
-    g_small[3].second(3)
-    begin_memory()
-    g_feed[1][0].second(2)
-    g_small[0].fourth()
-    g_small[1].fourth()
-    g_small[4].second(1)
-    g_small[0].last()
-    g_small[3].third(0)
-    g_feed[1][0].second(3)
-    g_small[3].third(1)
-    begin_third(0, 1)
-    g_small[1].last()
-    g_feed[0][0].second(1)
-    g_small[4].second(2)
-    g_small[4].second(3)
+    g_small[0].second(3)
     g_feed[0][0].second(2)
     g_feed[1][1].second(1)
+    begin_memory()
+    g_small[1].third(1)
+    g_small[2].second(3)
+    g_small[1].third(0)
+    g_small[3].second(3)
+    g_small[0].third(1)
+    g_small[0].third(0)
+    g_feed[2][0].third(0)
+    g_small[4].fourth()
+    g_small[2].third(1)
+    g_small[2].third(0)
+    g_feed[0][1].second(2)
     g_feed[0][0].second(3)
+    g_small[3].third(0)
+    g_small[0].fourth()
+    g_feed[2][0].third(1)
+    g_small[1].fourth()
+    g_small[3].third(1)
+    g_small[0].last()
+    g_small[1].last()
+    g_feed[1][0].second(1)
     g_feed[1][1].second(2)
-    g_small[2].third(1)
-    g_feed[1][1].second(3)
     layer.project(layer.qkv, lambda: layer.nrm[...], 0)
+    g_feed[0][1].second(3)
+    g_feed[2][0].fourth()
+    g_small[4].second(1)
     layer.self_forward(0, 2)
+    g_small[2].fourth()
+    g_feed[1][0].second(2)
     layer.self_forward(2, 4)
     away.start()
     g_feed[0][0].third(1)
-    g_small[4].third(0)
-    g_feed[1][0].third(1)
-    begin_third(2, 0)
-    g_small[3].fourth()
-    g_small[2].fourth()
-    g_feed[0][0].third(0)
     g_small[2].last()
-    g_feed[1][1].third(1)
-    g_feed[1][0].third(0)
     layer.add_after_self()
     top.start()
-    g_small[4].third(1)
-    g_feed[1][1].third(0)
+    g_feed[2][0].second(1)
+    g_feed[2][1].second(2)
     layer.norm_into(layer.after_self, 1)
     layer.project(layer.cq, lambda: layer.nrm[...], 4)
-    begin_third(2, 1)
-    g_small[3].last()
-    g_feed[0][0].fourth()
-    g_feed[0][0].last()
-    g_feed[1][0].fourth()
+    g_feed[1][0].second(3)
+    g_feed[1][1].second(3)
+    g_feed[0][1].third(0)
+    g_small[3].fourth()
+    g_small[4].second(2)
     end_memory()
     layer.memory_in()
-    g_feed[0][1].second(1)
+    g_small[3].last()
+    g_feed[2][1].second(3)
+    g_feed[0][0].third(0)
     layer.project(layer.mkv, layer.memory, 5)
-    g_feed[0][1].second(2)
-    g_feed[0][1].second(3)
-    g_feed[1][1].fourth()
-    g_small[4].fourth()
+    g_feed[0][1].third(1)
     away.wait()
     layer.cross_forward(0, 4)
-    g_feed[0][1].third(0)
-    g_feed[0][1].third(1)
-    g_feed[2][0].second(1)
+    g_feed[2][0].second(2)
+    g_feed[1][0].third(0)
+    g_feed[1][0].third(1)
+    g_small[4].second(3)
+    g_feed[1][1].third(1)
+    g_feed[1][1].third(0)
     layer.cross_forward(4, 8)
-    g_feed[2][0].second(2)
-    g_feed[1][1].last()
     g_small[4].last()
-    g_feed[2][1].second(1)
-    g_feed[2][1].second(2)
+    g_feed[0][1].fourth()
     layer.add_after_cross()
-    g_feed[0][1].fourth()
+    g_feed[0][0].fourth()
+    g_feed[2][1].third(1)
     layer.norm_into(layer.after_cross, 2)
     top.wait()
     layer.mask_top()
     layer.feed_start()
     drain_small()
-    g_feed[2][1].second(3)
     g_feed[0][1].last()
-    g_feed[2][0].second(3)
+    g_feed[2][1].third(0)
+    g_feed[0][0].last()
+    g_feed[1][0].fourth()
+    g_feed[1][1].fourth()
     each(g_feed[0], "drain")
     layer.feed_chunk(0)
-    g_feed[2][1].third(1)
-    r_feed[0][0].begin()
-    g_feed[2][1].third(0)
-    g_feed[2][0].third(0)
+    g_feed[2][0].second(3)
+    g_feed[1][1].last()
+    g_feed[2][1].fourth()
+    r_feed[0][1].begin()
     g_feed[1][0].last()
-    r_feed[0][1].begin()
-    g_feed[2][0].third(1)
     each(g_feed[1], "drain")
     layer.feed_chunk(1)
-    r_feed[0][0].second()
-    g_feed[2][1].fourth()
-    g_feed[2][0].fourth()
+    g_feed[2][0].last()
     r_feed[0][1].second()
-    g_feed[2][0].last()
+    r_feed[1][1].begin()
     r_feed[1][0].begin()
     g_feed[2][1].last()
-    r_feed[0][0].third(0)
     each(g_feed[2], "drain")
     layer.feed_chunk(2)
+    r_feed[1][1].second()
+    r_feed[2][1].begin()
     r_feed[0][1].third(1)
+    r_feed[1][0].second()
+    layer.third_back()
+    layer.output_back(7, layer.cm, t2)
+    r_feed[2][1].second()
     r_feed[2][0].begin()
+    r_small[0].begin()
+    layer.cross_back(0, 4)
+    r_feed[2][0].second()
+    r_feed[1][1].third(1)
+    r_small[0].second()
+    r_feed[1][0].third(1)
+    r_feed[1][1].third(0)
     r_feed[0][1].third(0)
-    layer.third_back()
-    r_feed[1][0].second()
-    r_feed[0][0].third(1)
-    layer.output_back(7, layer.cm, t2)
-    r_feed[2][0].second()
-    layer.cross_back(0, 4)
-    r_feed[1][0].third(0)
-    r_feed[1][1].begin()
-    r_feed[1][0].third(1)
-    r_feed[0][1].fourth()
+    r_feed[0][0].begin()
     layer.cross_back(4, 8)
     again.start()
-    r_feed[0][0].fourth()
-    r_feed[2][0].third(1)
-    r_feed[2][1].begin()
-    r_small[0].begin()
-    r_feed[2][0].third(0)
+    layer.memory_back()
+    layer.weight_grads(layer.mkv, layer.memory, 5)
+    r_feed[0][0].second()
+    r_feed[2][1].third(1)
+    r_small[4].begin()
+    r_small[0].relay(0)
+    r_feed[1][0].third(0)
+    layer.memory_out()
     layer.layer_out(t3)
     save_out.start()
-    layer.memory_back()
-    r_feed[1][0].fourth()
-    r_feed[1][1].second()
     layer.second_up()
-    r_small[0].second()
-    layer.weight_grads(layer.mkv, layer.memory, 5)
-    r_feed[2][0].fourth()
-    r_feed[2][1].second()
-    r_small[4].begin()
-    layer.memory_out()
-    r_small[0].third(0)
-    r_small[0].third(1)
+    r_feed[2][1].third(0)
+    r_small[4].second()
+    r_feed[2][0].third(1)
+    layer.second_back()
     send_memory()
+    layer.output_back(3, layer.sm, t2)
+    text.start()
     layer.norm_into(layer.after_self, 1)
     layer.weight_grads(layer.cq, lambda: layer.nrm[...], 4)
-    r_feed[1][1].third(0)
+    r_feed[1][1].fourth()
+    r_feed[0][1].fourth()
+    r_small[2].begin()
+    again.wait()
+    layer.self_back(0, 2)
+    r_small[4].third(0)
     r_small[1].begin()
-    layer.second_back()
-    r_small[4].second()
-    r_feed[1][1].third(1)
-    r_feed[0][1].fifth()
-    layer.output_back(3, layer.sm, t2)
-    text.start()
+    layer.self_back(2, 4)
+    r_small[4].third(1)
+    r_feed[2][1].fourth()
     text.wait()
     layer.norm_into(layer.sm, 0)
-    again.wait()
-    layer.self_back(0, 2)
+    layer.first_up()
+    r_feed[2][0].third(0)
+    layer.weight_grads(layer.qkv, lambda: layer.nrm[...], 0)
     r_small[1].second()
-    layer.self_back(2, 4)
-    r_small[4].third(0)
-    layer.first_up()
-    layer.weight_grads(layer.qkv, lambda: layer.nrm[...], 0)
-    r_small[4].third(1)
-    r_feed[2][1].third(0)
-    r_small[1].third(1)
-    r_feed[1][0].fifth()
     r_small[3].begin()
-    r_small[0].fourth()
-    r_feed[0][0].fifth()
-    r_small[1].third(0)
-    r_small[2].begin()
-    store(r_feed[1][0], fin_in)
-    r_feed[2][1].third(1)
     r_small[2].second()
-    store(r_feed[0][1], fin_out)
+    r_feed[0][0].relay(0)
+    r_small[3].second()
     save_out.wait()
     layer.first_back(layer.sm, t3)
     save_text.start()
-    r_feed[2][0].fifth()
+    r_feed[2][0].fourth()
+    r_small[0].relay(1)
+    r_feed[0][1].relay(0)
+    r_small[1].third(0)
     r_small[4].fourth()
-    r_feed[1][1].fourth()
-    r_small[3].second()
+    r_small[1].third(1)
+    r_small[3].third(0)
+    r_feed[1][0].fourth()
+    r_feed[2][0].relay(0)
+    r_small[3].third(1)
+    r_feed[2][1].relay(0)
+    r_feed[1][1].relay(0)
+    r_small[1].fourth()
+    r_feed[0][0].relay(1)
+    r_small[1].relay(0)
+    r_small[3].fourth()
+    r_feed[2][1].relay(1)
+    r_small[0].fourth()
+    r_small[2].third(1)
+    r_feed[0][0].fourth()
+    norm.start(0)
+    r_feed[1][0].relay(0)
+    r_small[4].relay(0)
     r_small[2].third(0)
-    r_small[2].third(1)
-    r_small[3].third(0)
-    r_small[1].fourth()
-    norm.start(0)
-    r_feed[2][1].fourth()
-    r_small[3].third(1)
+    r_feed[2][0].relay(1)
+    r_small[3].relay(0)
+    r_feed[2][1].fifth()
+    r_feed[0][0].third(1)
+    r_small[0].third(1)
+    r_feed[1][0].relay(1)
     r_small[2].fourth()
-    r_feed[1][1].fifth()
-    r_small[0].fifth()
-    store(r_feed[2][0], fin_in)
-    r_small[4].fifth()
-    store(r_small[0], fin_s)
-    r_small[3].fourth()
-    r_small[1].fifth()
     norm.finish(0)
     norm.start(1)
-    r_small[2].fifth()
+    r_feed[0][1].relay(1)
+    r_small[1].relay(1)
+    r_feed[0][0].third(0)
+    r_small[4].relay(1)
+    r_feed[1][1].relay(1)
+    r_feed[2][0].fifth()
+    r_feed[0][1].fifth()
+    store(r_feed[2][1], fin_out)
+    r_small[2].relay(0)
     norm.finish(1)
     norm.start(2)
+    store(r_feed[0][1], fin_out)
+    r_small[0].third(0)
+    r_small[3].relay(1)
+    r_feed[0][0].fifth()
+    r_small[1].fifth()
+    r_feed[1][1].fifth()
+    r_feed[1][0].fifth()
+    r_small[4].fifth()
+    r_small[2].relay(1)
+    r_small[0].fifth()
+    store(r_feed[0][0], fin_in)
+    store(r_small[1], fin_s)
+    store(r_feed[2][0], fin_in)
     store(r_feed[1][1], fin_out)
-    r_feed[2][1].fifth()
+    store(r_small[0], fin_s)
+    norm.finish(2)
     r_small[3].fifth()
-    store(r_feed[0][0], fin_in)
+    r_small[2].fifth()
+    store(r_feed[1][0], fin_in)
     store(r_small[4], fin_s)
+    store(r_small[3], fin_s)
     store(r_small[2], fin_s)
-    store(r_small[1], fin_s)
-    store(r_small[3], fin_s)
-    store(r_feed[2][1], fin_out)
-    norm.finish(2)
-
     save_text.wait()
     keep_back.wait()
     for k in range(1, 8):
@@ -1472,11 +1676,12 @@
         pltpu.VMEM((2 * depth, 4 * width), BF),
         pltpu.VMEM((2, half, 4 * depth), BF),
     ]
-    for _ in range(THIRDS):
-        scratch += reduce_bufs(1, half_in, lanes, 128)
-        scratch += reduce_bufs(1, half, units // 2, 256)
-    for a, b in SMALL_BACK:
-        scratch += reduce_bufs(b - a, half, lanes, 128)
+    for s in range(THIRDS):
+        n = 2 * s
+        scratch += reduce_bufs(1, half_in, lanes, 128, n in Z_FIRST_BACK)
+        scratch += reduce_bufs(1, half, units // 2, 256, n + 1 in Z_FIRST_BACK)
+    for n, (a, b) in enumerate(SMALL_BACK, 2 * THIRDS):
+        scratch += reduce_bufs(b - a, half, lanes, 128, n in Z_FIRST_BACK)
     scratch += [pltpu.VMEM((tokens, dmodel), BF) for _ in NAMES]
     scratch += [pltpu.VMEM((tokens, dmodel), F32) for _ in WIDE]
     stacks = [(3, tokens, dmodel), (1, tokens, dmodel), (2, mem_rows, dmodel)]

time: 227 us -> 210 us (0.925)
  Pallas kernels: 225 us -> 209 us
    pallas_call x1, Pallas kernels: 220 us -> 204 us  [whole(): pl.pallas_call(functools.partial(whole_kernel, images), out_shape=[jax.Sh...]
where the time goes in v1:
time: 210 us; the launch traced here: 209 us
  Pallas kernels  209 us (100%)
    pallas_call x1, Pallas kernels, whole(): pl.pallas_call(functools.partial(whole_kernel, images), out_shape=[jax.Sh...  204 us
    pallas_call x1, Pallas kernels, finish(): pl.pallas_call(finish_kernel, out_shape=[jax.ShapeDtypeStruct(s, F32) for...  4.79 us

profile of v1, /device:TPU:0, one launch (start us, length us, event | category | flops | bytes accessed | tf_op | source)
XLA Modules:
  0.0 209.4 jit_solution(15579925769237086448)
XLA Ops:
  0.7 203.8 %shard_map.339 = (bf16[8,2,48,384]{3,2,1,0:T(8,128)(2,1)}, bf16[3,2,64,384]{3,2,1,0:T(8,128)(2,1)}, bf16[3,2,48,512]{3,2,1,0:T(8,128)(2,1)}, bf16[512,768]{1,0:T...) custom-call(bf16[192,96]{1,0:T(8,128)(2,1)} %refs_0_.1, ...), custom_call_target="tpu_custom_call" | custom-call | tf_op jit(solution)/shard_map/pallas_call | solution.py:1706
  204.4 4.8 %shard_map.340 = (f32[192,96]{1,0:T(8,128)}, f32[192,96]{1,0:T(8,128)}, f32[192,96]{1,0:T(8,128)}, f32[192,96]{1,0:T(8,128)}, f32[192,96]{1,0:T(8,128)}, /*index...) custom-call(bf16[8,2,48,384]{3,2,1,0:T(8,128)(2,1)} %get-tuple-eleme, ...), custom_call_target="tpu_custom_call" | custom-call | tf_op jit(solution)/shard_map/pallas_call | solution.py:1760

commit v2 on v1

--- a/solution.py
+++ b/solution.py
@@ -1592,7 +1592,6 @@
     r_small[2].third(0)
     r_feed[2][0].relay(1)
     r_small[3].relay(0)
-    r_feed[2][1].fifth()
     r_feed[0][0].third(1)
     r_small[0].third(1)
     r_feed[1][0].relay(1)
@@ -1604,22 +1603,23 @@
     r_feed[0][0].third(0)
     r_small[4].relay(1)
     r_feed[1][1].relay(1)
-    r_feed[2][0].fifth()
-    r_feed[0][1].fifth()
-    store(r_feed[2][1], fin_out)
     r_small[2].relay(0)
     norm.finish(1)
     norm.start(2)
-    store(r_feed[0][1], fin_out)
     r_small[0].third(0)
     r_small[3].relay(1)
+    r_small[2].relay(1)
+    r_feed[0][1].fifth()
     r_feed[0][0].fifth()
-    r_small[1].fifth()
     r_feed[1][1].fifth()
     r_feed[1][0].fifth()
+    r_feed[2][0].fifth()
+    r_feed[2][1].fifth()
+    r_small[0].fifth()
+    r_small[1].fifth()
     r_small[4].fifth()
-    r_small[2].relay(1)
-    r_small[0].fifth()
+    store(r_feed[2][1], fin_out)
+    store(r_feed[0][1], fin_out)
     store(r_feed[0][0], fin_in)
     store(r_small[1], fin_s)
     store(r_feed[2][0], fin_in)

time: 210 us -> 209 us (level)
  no operation moved by 1% of the time
where the time goes in v2:
time: 209 us; the launch traced here: 208 us
  Pallas kernels  207 us (99%)
    pallas_call x1, Pallas kernels, whole(): pl.pallas_call(functools.partial(whole_kernel, images), out_shape=[jax.Sh...  202 us
    pallas_call x1, Pallas kernels, finish(): pl.pallas_call(finish_kernel, out_shape=[jax.ShapeDtypeStruct(s, F32) for...  4.79 us

profile of v2, /device:TPU:0, one launch (start us, length us, event | category | flops | bytes accessed | tf_op | source)
XLA Modules:
  0.0 207.8 jit_solution(13929670655396908651)
XLA Ops:
  0.7 202.2 %shard_map.339 = (bf16[8,2,48,384]{3,2,1,0:T(8,128)(2,1)}, bf16[3,2,64,384]{3,2,1,0:T(8,128)(2,1)}, bf16[3,2,48,512]{3,2,1,0:T(8,128)(2,1)}, bf16[512,768]{1,0:T...) custom-call(bf16[192,96]{1,0:T(8,128)(2,1)} %refs_0_.1, ...), custom_call_target="tpu_custom_call" | custom-call | tf_op jit(solution)/shard_map/pallas_call | solution.py:1706
  202.9 4.8 %shard_map.340 = (f32[192,96]{1,0:T(8,128)}, f32[192,96]{1,0:T(8,128)}, f32[192,96]{1,0:T(8,128)}, f32[192,96]{1,0:T(8,128)}, f32[192,96]{1,0:T(8,128)}, /*index...) custom-call(bf16[8,2,48,384]{3,2,1,0:T(8,128)(2,1)} %get-tuple-eleme, ...), custom_call_target="tpu_custom_call" | custom-call | tf_op jit(solution)/shard_map/pallas_call | solution.py:1760
